TPU v7x, 32 devices: a whole 2x2x4 slice. The times are simulated.
32 devices in a mesh: ens: 2 (over x), tile: 16 (over z, y, core).
Axes of the slice: x: 2, y: 2, z: 4, core: 2. Of those that a mesh axis runs over, the one named last changes fastest.
Arguments:
- final_adjoint: float32 [320, 32, 1024], P('ens', 'tile'), parts along dimension 0, may hold values from -0.5 to 1.5
- first_density: float32 [320, 32, 1024], P('ens', 'tile'), parts along dimension 0, may hold values from 0.05 to 2
- second_density: float32 [320, 32, 1024], P('ens', 'tile'), parts along dimension 0, may hold values from 0.05 to 2
- forage: float32 [4, 6, 32, 1024], P('ens', None, 'tile'), parts along dimension 0, may hold values from 5 to 50
- preference: float32 [32, 6], P('ens'), parts along dimension 0, may hold values from 0.02 to 0.3
- base_mortality: float32 [160], replicated, may hold values from 0.01 to 0.5
- age_class: int32 [160], replicated, may hold values from 0 to 15, never falling along the last dimension, each value on 1 to 20 neighbouring positions
- land_mask: int32 [32, 1024], P('tile'), may hold values 0 or 1
- east_velocity: float32 [32, 1024], P('tile'), may hold values from -0.1 to 0.1
- north_velocity: float32 [32, 1024], P('tile'), may hold values from -0.1 to 0.1
Outputs:
- initial_adjoint: float32 [320, 32, 1024], P('ens', 'tile'), parts along dimension 0
- forage_sensitivity: float32 [4, 6, 32, 1024], P('ens', None, 'tile'), parts along dimension 0
- preference_gradient: float32 [32, 6], P('ens'), parts along dimension 0
There are 2 independent parts, one for each index of `ens`. A program takes and returns all parts, laid end to end along the dimension named above; an argument that names none is the same for every part. Nothing has to cross between parts.
Inputs may be any that keep to these rules, and one draw needn't show every extreme that they name: `age_class`: never falls along the cohorts; every class holds 1 to 20 cohorts, one exactly that many.
All inputs are finite; a program needn't handle non-finite values. No bound on the sum of `land_mask` on one device may be relied on, other than what follows from the above.
Results may differ from a plain program's by a relative error of at most 0.00011.
Values sent between devices are 32-bit elements; how exact they have to be, the bound alone decides.
A program may use at most 64 MiB of HBM per device.

v0:
```python
import jax
import jax.numpy as jnp
from jax import lax
from jax.sharding import PartitionSpec as P

SUBSTEPS = 4


HIGH = lax.Precision.HIGHEST


def with_halo(cells, sides, width):
    for axis, dim in sides:
        count = lax.axis_size(axis)
        ends = count - 1
        head = lax.slice_in_dim(cells, 0, width, axis=dim)
        tail = lax.slice_in_dim(cells, cells.shape[dim] - width, cells.shape[dim], axis=dim)
        cells = jnp.concatenate(
            [
                lax.ppermute(tail, axis, [(i, (i + 1) % count) for i in range(ends)]),
                cells,
                lax.ppermute(head, axis, [((i + 1) % count, i) for i in range(ends)]),
            ],
            axis=dim,
        )
    return cells


def make_rates(extended):
    mask = extended[0]
    centre = mask[1:-1]
    east_velocity = extended[1][1:-1]
    north_velocity = extended[2][1:-1]
    rate_n = centre * mask[:-2] * (0.1 + jnp.maximum(north_velocity, 0.0))
    rate_s = centre * mask[2:] * (0.1 + jnp.maximum(-north_velocity, 0.0))
    rate_e = centre * jnp.roll(centre, -1, axis=1) * (0.1 + jnp.maximum(east_velocity, 0.0))
    rate_w = centre * jnp.roll(centre, 1, axis=1) * (0.1 + jnp.maximum(-east_velocity, 0.0))
    keep = 1.0 - rate_n - rate_s - rate_e - rate_w
    return (keep, rate_n, rate_s, rate_e, rate_w)


def transpose_step(padded, first_row, rates):
    count = padded.shape[1] - 2
    begin = first_row + 1
    keep, rate_n, rate_s, rate_e, rate_w = [r[begin : begin + count] for r in rates]
    centre = padded[:, 1:-1]
    return (
        keep * centre
        + rate_n * padded[:, :-2]
        + rate_s * padded[:, 2:]
        + rate_e * jnp.roll(centre, -1, axis=2)
        + rate_w * jnp.roll(centre, 1, axis=2)
    )


def transported(incoming, rates):
    carried = incoming

    def one_step(index, field):
        wide = with_halo(field, (("tile", 1),), 1)
        return transpose_step(wide, 0, rates)

    carried = lax.fori_loop(0, SUBSTEPS, one_step, carried)
    return carried


def month_adjoint(incoming, density, food, pref_rows, base_mortality, rates, onehot):
    carried = transported(incoming, rates)
    cohorts = carried.shape[0]
    aged = jnp.concatenate([carried[1:], carried[cohorts - 1 :]], axis=0).reshape(cohorts, -1)
    dens = density.reshape(cohorts, -1)
    feed = food.reshape(food.shape[0], -1)
    demand = jnp.dot(pref_rows.T, dens, precision=HIGH)
    total = feed + demand
    short = demand / total
    survival = jnp.exp(-(base_mortality[:, None] + jnp.dot(pref_rows, short, precision=HIGH)))
    grown = survival * dens
    adj_mort = -aged * grown
    adj_ratio = -jnp.dot(pref_rows.T, adj_mort, precision=HIGH)
    squared = total * total
    adj_demand = -adj_ratio * feed / squared
    sensitivity = adj_ratio * demand * feed / squared
    outgoing = aged * survival + jnp.dot(pref_rows, adj_demand, precision=HIGH)
    cohort_grad = jnp.dot(adj_mort, short.T, precision=HIGH) + jnp.dot(
        dens, adj_demand.T, precision=HIGH
    )
    class_grad = jnp.dot(onehot, cohort_grad, precision=HIGH)
    return (outgoing.reshape(density.shape), sensitivity.reshape(food.shape), class_grad)


def shards(
    final_adjoint,
    first_density,
    second_density,
    forage,
    preference,
    base_mortality,
    age_class,
    land_mask,
    east_velocity,
    north_velocity,
):
    classes = preference.shape[0]
    onehot = (age_class[None, :] == jnp.arange(classes, dtype=jnp.int32)[:, None]).astype(
        jnp.float32
    )
    pref_rows = jnp.dot(onehot.T, preference, precision=HIGH)
    fields = jnp.stack([land_mask.astype(jnp.float32), east_velocity, north_velocity], axis=0)
    extended = with_halo(fields, (("tile", 1),), 2)
    rates = make_rates(extended)
    cells = land_mask.shape[0] * lax.axis_size("tile") * land_mask.shape[1]
    middle, sens_two, grad_two = month_adjoint(
        final_adjoint, second_density, forage[1], pref_rows, base_mortality, rates, onehot
    )

    def month_total(local_grad):
        return lax.psum(local_grad, "tile")

    total_two = month_total(grad_two)
    initial, sens_one, grad_one = month_adjoint(
        middle, first_density, forage[0], pref_rows, base_mortality, rates, onehot
    )
    summed = month_total(grad_one) + total_two
    return (initial, jnp.stack([sens_one, sens_two], axis=0), summed / cells)


def solution(mesh):
    in_specs = (
        P("ens", "tile", None),
        P("ens", "tile", None),
        P("ens", "tile", None),
        P("ens", None, "tile", None),
        P("ens", None),
        P(),
        P(),
        P("tile", None),
        P("tile", None),
        P("tile", None),
    )
    out_specs = (P("ens", "tile", None), P("ens", None, "tile", None), P("ens", None))
    return jax.shard_map(shards, mesh=mesh, in_specs=in_specs, out_specs=out_specs, check_vma=False)
```

profile of v0, /device:TPU:0, one launch (start us, length us, event | category | flops | bytes accessed | tf_op | source)
XLA Modules:
  0.0 273.3 jit_solution(4688281940485553662)
XLA Ops:
  1.4 2.4 collective-permute-start.4
  8.8 2.4 fusion.15
  11.2 2.4 fusion.13
  14.5 94.6 %while.20 = (s32[]{:T(128)}, f32[160,2,1024]{2,1,0:T(2,128)S(1)}, f32[4,1024]{1,0:T(4,128)}, f32[4,1024]{1,0:T(4,128)}, f32[4,1024]{1,0:T(4,128)}, /*index=5*/f32[4,1024]{1,0:T(4,128)}, f32[4,1024]{1,0:T(4,128)}, s32[]{:T(128)}) while((s32[]{:T(128)}, f32[160,2,1024]{2,1,0:T(2,128)S(1)}, f32[4,1024]{1,0:T(4,128)}, f32[4,1024]{1,0:T(4,128)}, ...), condition=%wide.region_1.2_spmd, body=%wide.region_0.1_spmd.sunk | while | flops 4259842 | bytes 22864288 | solution.py:63
  17.4 6.6 %collective-permute-start.1 = (f32[160,1,1024]{2,1,0:T(1,128)S(1)}, f32[160,1,1024]{2,1,0:T(1,128)}, u32[]{:S(2)}, u32[]{:S(2)}) collective-permute-start(f32[160,1,1024]{2,1,0:T(1,128)S(1)} %get-tuple-element.228), channel_id=1, source_target_pairs={{0,1},{1,2},{2,3},{3,4},{4,5},{5,6},{6,7},{7,8},{8,9},{9,10},{10,1... | collective-permute-start | bytes 1966088 | tf_op jit(solution)/shard_map/while/body/eval_jaxpr/ppermute | solution.py:20
  26.7 1.8 fusion.74
  28.6 5.9 %fusion.75 = f32[160,2,1024]{2,1,0:T(2,128)S(1)} fusion(f32[160,1,1024]{2,1,0:T(1,128)S(1)} %collective-permute-done, f32[160,2,1024]{2,1,0:T(2,128)S(1)} %copy.37, f32[160,1,1024]{2,1,0:T(1,128)} %collective-permute-done.1, f32[160,2,1]{2,1,0:T(2,128)S(1)} %get-tuple-element.229, f32[160,2,1023]{2,1,0:T(2,128)S(1)} %get-tuple-element.230, ...), kind=kLoop, calls=%fused_computation.4.clone.1 | loop fusion | flops 4259840 | bytes 6594560 | tf_op jit(solution)/shard_map/while/body/eval_jaxpr/add | solution.py:48
  37.4 13.3 %collective-permute-start.1 = (f32[160,1,1024]{2,1,0:T(1,128)S(1)}, f32[160,1,1024]{2,1,0:T(1,128)}, u32[]{:S(2)}, u32[]{:S(2)}) collective-permute-start(f32[160,1,1024]{2,1,0:T(1,128)S(1)} %get-tuple-element.228), channel_id=1, source_target_pairs={{0,1},{1,2},{2,3},{3,4},{4,5},{5,6},{6,7},{7,8},{8,9},{9,10},{10,1... | collective-permute-start | bytes 1966088 | tf_op jit(solution)/shard_map/while/body/eval_jaxpr/ppermute | solution.py:20
  53.4 1.8 fusion.74
  55.2 5.9 %fusion.75 = f32[160,2,1024]{2,1,0:T(2,128)S(1)} fusion(f32[160,1,1024]{2,1,0:T(1,128)S(1)} %collective-permute-done, f32[160,2,1024]{2,1,0:T(2,128)S(1)} %copy.37, f32[160,1,1024]{2,1,0:T(1,128)} %collective-permute-done.1, f32[160,2,1]{2,1,0:T(2,128)S(1)} %get-tuple-element.229, f32[160,2,1023]{2,1,0:T(2,128)S(1)} %get-tuple-element.230, ...), kind=kLoop, calls=%fused_computation.4.clone.1 | loop fusion | flops 4259840 | bytes 6594560 | tf_op jit(solution)/shard_map/while/body/eval_jaxpr/add | solution.py:48
  64.0 9.1 %collective-permute-start.1 = (f32[160,1,1024]{2,1,0:T(1,128)S(1)}, f32[160,1,1024]{2,1,0:T(1,128)}, u32[]{:S(2)}, u32[]{:S(2)}) collective-permute-start(f32[160,1,1024]{2,1,0:T(1,128)S(1)} %get-tuple-element.228), channel_id=1, source_target_pairs={{0,1},{1,2},{2,3},{3,4},{4,5},{5,6},{6,7},{7,8},{8,9},{9,10},{10,1... | collective-permute-start | bytes 1966088 | tf_op jit(solution)/shard_map/while/body/eval_jaxpr/ppermute | solution.py:20
  75.8 1.8 fusion.74
  77.7 5.9 %fusion.75 = f32[160,2,1024]{2,1,0:T(2,128)S(1)} fusion(f32[160,1,1024]{2,1,0:T(1,128)S(1)} %collective-permute-done, f32[160,2,1024]{2,1,0:T(2,128)S(1)} %copy.37, f32[160,1,1024]{2,1,0:T(1,128)} %collective-permute-done.1, f32[160,2,1]{2,1,0:T(2,128)S(1)} %get-tuple-element.229, f32[160,2,1023]{2,1,0:T(2,128)S(1)} %get-tuple-element.230, ...), kind=kLoop, calls=%fused_computation.4.clone.1 | loop fusion | flops 4259840 | bytes 6594560 | tf_op jit(solution)/shard_map/while/body/eval_jaxpr/add | solution.py:48
  86.5 12.1 %collective-permute-start.1 = (f32[160,1,1024]{2,1,0:T(1,128)S(1)}, f32[160,1,1024]{2,1,0:T(1,128)}, u32[]{:S(2)}, u32[]{:S(2)}) collective-permute-start(f32[160,1,1024]{2,1,0:T(1,128)S(1)} %get-tuple-element.228), channel_id=1, source_target_pairs={{0,1},{1,2},{2,3},{3,4},{4,5},{5,6},{6,7},{7,8},{8,9},{9,10},{10,1... | collective-permute-start | bytes 1966088 | tf_op jit(solution)/shard_map/while/body/eval_jaxpr/ppermute | solution.py:20
  101.4 1.8 fusion.74
  103.2 5.9 %fusion.75 = f32[160,2,1024]{2,1,0:T(2,128)S(1)} fusion(f32[160,1,1024]{2,1,0:T(1,128)S(1)} %collective-permute-done, f32[160,2,1024]{2,1,0:T(2,128)S(1)} %copy.37, f32[160,1,1024]{2,1,0:T(1,128)} %collective-permute-done.1, f32[160,2,1]{2,1,0:T(2,128)S(1)} %get-tuple-element.229, f32[160,2,1023]{2,1,0:T(2,128)S(1)} %get-tuple-element.230, ...), kind=kLoop, calls=%fused_computation.4.clone.1 | loop fusion | flops 4259840 | bytes 6594560 | tf_op jit(solution)/shard_map/while/body/eval_jaxpr/add | solution.py:48
  111.9 1.8 fusion.31
  118.4 96.1 %while.21 = (s32[]{:T(128)}, f32[160,2,1024]{2,1,0:T(2,128)S(1)}, f32[4,1024]{1,0:T(4,128)}, f32[4,1024]{1,0:T(4,128)}, f32[4,1024]{1,0:T(4,128)}, /*index=5*/f32[4,1024]{1,0:T(4,128)}, f32[4,1024]{1,0:T(4,128)}, s32[]{:T(128)}) while((s32[]{:T(128)}, f32[160,2,1024]{2,1,0:T(2,128)S(1)}, f32[4,1024]{1,0:T(4,128)}, f32[4,1024]{1,0:T(4,128)}, ...), condition=%wide.region_3.4_spmd, body=%wide.region_2.3_spmd.sunk | while | flops 4259842 | bytes 22864288 | solution.py:63
  121.4 9.1 %collective-permute-start.3 = (f32[160,1,1024]{2,1,0:T(1,128)S(1)}, f32[160,1,1024]{2,1,0:T(1,128)}, u32[]{:S(2)}, u32[]{:S(2)}) collective-permute-start(f32[160,1,1024]{2,1,0:T(1,128)S(1)} %get-tuple-element.241), channel_id=1, source_target_pairs={{0,1},{1,2},{2,3},{3,4},{4,5},{5,6},{6,7},{7,8},{8,9},{9,10},{10,1... | collective-permute-start | bytes 1966088 | tf_op jit(solution)/shard_map/while/body/eval_jaxpr/ppermute | solution.py:20
  133.2 1.8 fusion.78
  135.1 5.9 %fusion.79 = f32[160,2,1024]{2,1,0:T(2,128)S(1)} fusion(f32[160,1,1024]{2,1,0:T(1,128)S(1)} %collective-permute-done.2, f32[160,2,1024]{2,1,0:T(2,128)S(1)} %copy.38, f32[160,1,1024]{2,1,0:T(1,128)} %collective-permute-done.3, f32[160,2,1]{2,1,0:T(2,128)S(1)} %get-tuple-element.242, f32[160,2,1023]{2,1,0:T(2,128)S(1)} %get-tuple-element.243, ...), kind=kLoop, calls=%fused_computation.14.clone.1 | loop fusion | flops 4259840 | bytes 6594560 | tf_op jit(solution)/shard_map/while/body/eval_jaxpr/add | solution.py:48
  143.9 12.2 %collective-permute-start.3 = (f32[160,1,1024]{2,1,0:T(1,128)S(1)}, f32[160,1,1024]{2,1,0:T(1,128)}, u32[]{:S(2)}, u32[]{:S(2)}) collective-permute-start(f32[160,1,1024]{2,1,0:T(1,128)S(1)} %get-tuple-element.241), channel_id=1, source_target_pairs={{0,1},{1,2},{2,3},{3,4},{4,5},{5,6},{6,7},{7,8},{8,9},{9,10},{10,1... | collective-permute-start | bytes 1966088 | tf_op jit(solution)/shard_map/while/body/eval_jaxpr/ppermute | solution.py:20
  158.7 1.8 fusion.78
  160.6 5.9 %fusion.79 = f32[160,2,1024]{2,1,0:T(2,128)S(1)} fusion(f32[160,1,1024]{2,1,0:T(1,128)S(1)} %collective-permute-done.2, f32[160,2,1024]{2,1,0:T(2,128)S(1)} %copy.38, f32[160,1,1024]{2,1,0:T(1,128)} %collective-permute-done.3, f32[160,2,1]{2,1,0:T(2,128)S(1)} %get-tuple-element.242, f32[160,2,1023]{2,1,0:T(2,128)S(1)} %get-tuple-element.243, ...), kind=kLoop, calls=%fused_computation.14.clone.1 | loop fusion | flops 4259840 | bytes 6594560 | tf_op jit(solution)/shard_map/while/body/eval_jaxpr/add | solution.py:48
  169.4 9.2 %collective-permute-start.3 = (f32[160,1,1024]{2,1,0:T(1,128)S(1)}, f32[160,1,1024]{2,1,0:T(1,128)}, u32[]{:S(2)}, u32[]{:S(2)}) collective-permute-start(f32[160,1,1024]{2,1,0:T(1,128)S(1)} %get-tuple-element.241), channel_id=1, source_target_pairs={{0,1},{1,2},{2,3},{3,4},{4,5},{5,6},{6,7},{7,8},{8,9},{9,10},{10,1... | collective-permute-start | bytes 1966088 | tf_op jit(solution)/shard_map/while/body/eval_jaxpr/ppermute | solution.py:20
  181.3 1.8 fusion.78
  183.1 5.9 %fusion.79 = f32[160,2,1024]{2,1,0:T(2,128)S(1)} fusion(f32[160,1,1024]{2,1,0:T(1,128)S(1)} %collective-permute-done.2, f32[160,2,1024]{2,1,0:T(2,128)S(1)} %copy.38, f32[160,1,1024]{2,1,0:T(1,128)} %collective-permute-done.3, f32[160,2,1]{2,1,0:T(2,128)S(1)} %get-tuple-element.242, f32[160,2,1023]{2,1,0:T(2,128)S(1)} %get-tuple-element.243, ...), kind=kLoop, calls=%fused_computation.14.clone.1 | loop fusion | flops 4259840 | bytes 6594560 | tf_op jit(solution)/shard_map/while/body/eval_jaxpr/add | solution.py:48
  191.9 12.1 %collective-permute-start.3 = (f32[160,1,1024]{2,1,0:T(1,128)S(1)}, f32[160,1,1024]{2,1,0:T(1,128)}, u32[]{:S(2)}, u32[]{:S(2)}) collective-permute-start(f32[160,1,1024]{2,1,0:T(1,128)S(1)} %get-tuple-element.241), channel_id=1, source_target_pairs={{0,1},{1,2},{2,3},{3,4},{4,5},{5,6},{6,7},{7,8},{8,9},{9,10},{10,1... | collective-permute-start | bytes 1966088 | tf_op jit(solution)/shard_map/while/body/eval_jaxpr/ppermute | solution.py:20
  206.7 1.8 fusion.78
  208.5 5.9 %fusion.79 = f32[160,2,1024]{2,1,0:T(2,128)S(1)} fusion(f32[160,1,1024]{2,1,0:T(1,128)S(1)} %collective-permute-done.2, f32[160,2,1024]{2,1,0:T(2,128)S(1)} %copy.38, f32[160,1,1024]{2,1,0:T(1,128)} %collective-permute-done.3, f32[160,2,1]{2,1,0:T(2,128)S(1)} %get-tuple-element.242, f32[160,2,1023]{2,1,0:T(2,128)S(1)} %get-tuple-element.243, ...), kind=kLoop, calls=%fused_computation.14.clone.1 | loop fusion | flops 4259840 | bytes 6594560 | tf_op jit(solution)/shard_map/while/body/eval_jaxpr/add | solution.py:48
  224.0 45.8 %psum.16 = f32[16,6]{0,1:T(8,128)S(1)} all-reduce(f32[16,6]{0,1:T(8,128)S(1)} %convolution_add_fusion.4), channel_id=1, replica_groups=mesh['ens'=2,'tile'=16] {'tile'}, use_global_device_ids=true, to_apply=%region_4.5 | all-reduce | flops 96 | bytes 768 | tf_op jit(solution)/shard_map/psum | solution.py:117
  270.4 2.2 reshape.64
  (319 shorter events, 68.1 us)
Async XLA Ops:
  1.4 12.2 %collective-permute-start.4 = (f32[3,2,1024]{2,1,0:T(2,128)S(1)}, f32[3,2,1024]{2,1,0:T(2,128)S(1)}, u32[]{:S(2)}, u32[]{:S(2)}) collective-permute-start(f32[3,2,1024]{2,1,0:T(2,128)S(1)} %pad_maximum_fusion.7), channel_id=1, source_target_pairs={{0,1},{1,2},{2,3},{3,4},{4,5},{5,6},{6,7},{7,8},{8,9},{9,10},{10,1... | collective-permute-start | bytes 73736 | tf_op jit(solution)/shard_map/ppermute | solution.py:20
  3.8 9.8 %collective-permute-start.5 = (f32[3,2,1024]{2,1,0:T(2,128)S(1)}, f32[3,2,1024]{2,1,0:T(2,128)S(1)}, u32[]{:S(2)}, u32[]{:S(2)}) collective-permute-start(f32[3,2,1024]{2,1,0:T(2,128)S(1)} %pad_maximum_fusion.7), channel_id=1, source_target_pairs={{1,0},{2,1},{3,2},{4,3},{5,4},{6,5},{7,6},{8,7},{9,8},{10,9},{11,1... | collective-permute-start | bytes 73736 | tf_op jit(solution)/shard_map/ppermute | solution.py:22
  16.1 12.4 %collective-permute-start = (f32[160,1,1024]{2,1,0:T(1,128)S(1)}, f32[160,1,1024]{2,1,0:T(1,128)S(1)}, u32[]{:S(2)}, u32[]{:S(2)}) collective-permute-start(f32[160,1,1024]{2,1,0:T(1,128)S(1)} %get-tuple-element.227), channel_id=1, source_target_pairs={{1,0},{2,1},{3,2},{4,3},{5,4},{6,5},{7,6},{8,7},{9,8},{10,9},{11,1... | collective-permute-start | bytes 1966088 | tf_op jit(solution)/shard_map/while/body/eval_jaxpr/ppermute | solution.py:22
  17.4 11.2 %collective-permute-start.1 = (f32[160,1,1024]{2,1,0:T(1,128)S(1)}, f32[160,1,1024]{2,1,0:T(1,128)}, u32[]{:S(2)}, u32[]{:S(2)}) collective-permute-start(f32[160,1,1024]{2,1,0:T(1,128)S(1)} %get-tuple-element.228), channel_id=1, source_target_pairs={{0,1},{1,2},{2,3},{3,4},{4,5},{5,6},{6,7},{7,8},{8,9},{9,10},{10,1... | collective-permute-start | bytes 1966088 | tf_op jit(solution)/shard_map/while/body/eval_jaxpr/ppermute | solution.py:20
  35.0 15.7 %copy-start.32 = (f32[4,1024]{1,0:T(4,128)S(1)}, f32[4,1024]{1,0:T(4,128)}, u32[]{:S(2)}) copy-start(f32[4,1024]{1,0:T(4,128)} %get-tuple-element.268) | copy-start | bytes 49156 | tf_op jit(solution)/shard_map/while
  35.0 15.7 %copy-start.30 = (f32[4,1024]{1,0:T(4,128)S(1)}, f32[4,1024]{1,0:T(4,128)}, u32[]{:S(2)}) copy-start(f32[4,1024]{1,0:T(4,128)} %get-tuple-element.267) | copy-start | bytes 49156 | tf_op jit(solution)/shard_map/while
  35.0 16.3 %copy-start.28 = (f32[4,1024]{1,0:T(4,128)S(1)}, f32[4,1024]{1,0:T(4,128)}, u32[]{:S(2)}) copy-start(f32[4,1024]{1,0:T(4,128)} %get-tuple-element.266) | copy-start | bytes 49156 | tf_op jit(solution)/shard_map/while
  35.0 16.9 %copy-start.26 = (f32[4,1024]{1,0:T(4,128)S(1)}, f32[4,1024]{1,0:T(4,128)}, u32[]{:S(2)}) copy-start(f32[4,1024]{1,0:T(4,128)} %get-tuple-element.265) | copy-start | bytes 49156 | tf_op jit(solution)/shard_map/while
  35.0 17.5 %copy-start.24 = (f32[4,1024]{1,0:T(4,128)S(1)}, f32[4,1024]{1,0:T(4,128)}, u32[]{:S(2)}) copy-start(f32[4,1024]{1,0:T(4,128)} %get-tuple-element.264) | copy-start | bytes 49156 | tf_op jit(solution)/shard_map/while
  36.1 19.1 %collective-permute-start = (f32[160,1,1024]{2,1,0:T(1,128)S(1)}, f32[160,1,1024]{2,1,0:T(1,128)S(1)}, u32[]{:S(2)}, u32[]{:S(2)}) collective-permute-start(f32[160,1,1024]{2,1,0:T(1,128)S(1)} %get-tuple-element.227), channel_id=1, source_target_pairs={{1,0},{2,1},{3,2},{4,3},{5,4},{6,5},{7,6},{8,7},{9,8},{10,9},{11,1... | collective-permute-start | bytes 1966088 | tf_op jit(solution)/shard_map/while/body/eval_jaxpr/ppermute | solution.py:22
  37.4 17.8 %collective-permute-start.1 = (f32[160,1,1024]{2,1,0:T(1,128)S(1)}, f32[160,1,1024]{2,1,0:T(1,128)}, u32[]{:S(2)}, u32[]{:S(2)}) collective-permute-start(f32[160,1,1024]{2,1,0:T(1,128)S(1)} %get-tuple-element.228), channel_id=1, source_target_pairs={{0,1},{1,2},{2,3},{3,4},{4,5},{5,6},{6,7},{7,8},{8,9},{9,10},{10,1... | collective-permute-start | bytes 1966088 | tf_op jit(solution)/shard_map/while/body/eval_jaxpr/ppermute | solution.py:20
  62.7 14.9 %collective-permute-start = (f32[160,1,1024]{2,1,0:T(1,128)S(1)}, f32[160,1,1024]{2,1,0:T(1,128)S(1)}, u32[]{:S(2)}, u32[]{:S(2)}) collective-permute-start(f32[160,1,1024]{2,1,0:T(1,128)S(1)} %get-tuple-element.227), channel_id=1, source_target_pairs={{1,0},{2,1},{3,2},{4,3},{5,4},{6,5},{7,6},{8,7},{9,8},{10,9},{11,1... | collective-permute-start | bytes 1966088 | tf_op jit(solution)/shard_map/while/body/eval_jaxpr/ppermute | solution.py:22
  64.0 13.6 %collective-permute-start.1 = (f32[160,1,1024]{2,1,0:T(1,128)S(1)}, f32[160,1,1024]{2,1,0:T(1,128)}, u32[]{:S(2)}, u32[]{:S(2)}) collective-permute-start(f32[160,1,1024]{2,1,0:T(1,128)S(1)} %get-tuple-element.228), channel_id=1, source_target_pairs={{0,1},{1,2},{2,3},{3,4},{4,5},{5,6},{6,7},{7,8},{8,9},{9,10},{10,1... | collective-permute-start | bytes 1966088 | tf_op jit(solution)/shard_map/while/body/eval_jaxpr/ppermute | solution.py:20
  84.2 15.1 %copy-start.28 = (f32[4,1024]{1,0:T(4,128)S(1)}, f32[4,1024]{1,0:T(4,128)}, u32[]{:S(2)}) copy-start(f32[4,1024]{1,0:T(4,128)} %get-tuple-element.266) | copy-start | bytes 49156 | tf_op jit(solution)/shard_map/while
  84.2 15.7 %copy-start.26 = (f32[4,1024]{1,0:T(4,128)S(1)}, f32[4,1024]{1,0:T(4,128)}, u32[]{:S(2)}) copy-start(f32[4,1024]{1,0:T(4,128)} %get-tuple-element.265) | copy-start | bytes 49156 | tf_op jit(solution)/shard_map/while
  84.2 16.3 %copy-start.24 = (f32[4,1024]{1,0:T(4,128)S(1)}, f32[4,1024]{1,0:T(4,128)}, u32[]{:S(2)}) copy-start(f32[4,1024]{1,0:T(4,128)} %get-tuple-element.264) | copy-start | bytes 49156 | tf_op jit(solution)/shard_map/while
  85.2 17.9 %collective-permute-start = (f32[160,1,1024]{2,1,0:T(1,128)S(1)}, f32[160,1,1024]{2,1,0:T(1,128)S(1)}, u32[]{:S(2)}, u32[]{:S(2)}) collective-permute-start(f32[160,1,1024]{2,1,0:T(1,128)S(1)} %get-tuple-element.227), channel_id=1, source_target_pairs={{1,0},{2,1},{3,2},{4,3},{5,4},{6,5},{7,6},{8,7},{9,8},{10,9},{11,1... | collective-permute-start | bytes 1966088 | tf_op jit(solution)/shard_map/while/body/eval_jaxpr/ppermute | solution.py:22
  86.5 16.7 %collective-permute-start.1 = (f32[160,1,1024]{2,1,0:T(1,128)S(1)}, f32[160,1,1024]{2,1,0:T(1,128)}, u32[]{:S(2)}, u32[]{:S(2)}) collective-permute-start(f32[160,1,1024]{2,1,0:T(1,128)S(1)} %get-tuple-element.228), channel_id=1, source_target_pairs={{0,1},{1,2},{2,3},{3,4},{4,5},{5,6},{6,7},{7,8},{8,9},{9,10},{10,1... | collective-permute-start | bytes 1966088 | tf_op jit(solution)/shard_map/while/body/eval_jaxpr/ppermute | solution.py:20
  120.1 14.9 %collective-permute-start.2 = (f32[160,1,1024]{2,1,0:T(1,128)S(1)}, f32[160,1,1024]{2,1,0:T(1,128)S(1)}, u32[]{:S(2)}, u32[]{:S(2)}) collective-permute-start(f32[160,1,1024]{2,1,0:T(1,128)S(1)} %get-tuple-element.240), channel_id=1, source_target_pairs={{1,0},{2,1},{3,2},{4,3},{5,4},{6,5},{7,6},{8,7},{9,8},{10,9},{11,1... | collective-permute-start | bytes 1966088 | tf_op jit(solution)/shard_map/while/body/eval_jaxpr/ppermute | solution.py:22
  121.4 13.6 %collective-permute-start.3 = (f32[160,1,1024]{2,1,0:T(1,128)S(1)}, f32[160,1,1024]{2,1,0:T(1,128)}, u32[]{:S(2)}, u32[]{:S(2)}) collective-permute-start(f32[160,1,1024]{2,1,0:T(1,128)S(1)} %get-tuple-element.241), channel_id=1, source_target_pairs={{0,1},{1,2},{2,3},{3,4},{4,5},{5,6},{6,7},{7,8},{8,9},{9,10},{10,1... | collective-permute-start | bytes 1966088 | tf_op jit(solution)/shard_map/while/body/eval_jaxpr/ppermute | solution.py:20
  141.5 15.1 %copy-start.29 = (f32[4,1024]{1,0:T(4,128)S(1)}, f32[4,1024]{1,0:T(4,128)}, u32[]{:S(2)}) copy-start(f32[4,1024]{1,0:T(4,128)} %get-tuple-element.290) | copy-start | bytes 49156 | tf_op jit(solution)/shard_map/while
  141.5 15.7 %copy-start.27 = (f32[4,1024]{1,0:T(4,128)S(1)}, f32[4,1024]{1,0:T(4,128)}, u32[]{:S(2)}) copy-start(f32[4,1024]{1,0:T(4,128)} %get-tuple-element.289) | copy-start | bytes 49156 | tf_op jit(solution)/shard_map/while
  141.5 16.3 %copy-start.25 = (f32[4,1024]{1,0:T(4,128)S(1)}, f32[4,1024]{1,0:T(4,128)}, u32[]{:S(2)}) copy-start(f32[4,1024]{1,0:T(4,128)} %get-tuple-element.288) | copy-start | bytes 49156 | tf_op jit(solution)/shard_map/while
  142.6 17.9 %collective-permute-start.2 = (f32[160,1,1024]{2,1,0:T(1,128)S(1)}, f32[160,1,1024]{2,1,0:T(1,128)S(1)}, u32[]{:S(2)}, u32[]{:S(2)}) collective-permute-start(f32[160,1,1024]{2,1,0:T(1,128)S(1)} %get-tuple-element.240), channel_id=1, source_target_pairs={{1,0},{2,1},{3,2},{4,3},{5,4},{6,5},{7,6},{8,7},{9,8},{10,9},{11,1... | collective-permute-start | bytes 1966088 | tf_op jit(solution)/shard_map/while/body/eval_jaxpr/ppermute | solution.py:22
  143.9 16.7 %collective-permute-start.3 = (f32[160,1,1024]{2,1,0:T(1,128)S(1)}, f32[160,1,1024]{2,1,0:T(1,128)}, u32[]{:S(2)}, u32[]{:S(2)}) collective-permute-start(f32[160,1,1024]{2,1,0:T(1,128)S(1)} %get-tuple-element.241), channel_id=1, source_target_pairs={{0,1},{1,2},{2,3},{3,4},{4,5},{5,6},{6,7},{7,8},{8,9},{9,10},{10,1... | collective-permute-start | bytes 1966088 | tf_op jit(solution)/shard_map/while/body/eval_jaxpr/ppermute | solution.py:20
  168.1 15.0 %collective-permute-start.2 = (f32[160,1,1024]{2,1,0:T(1,128)S(1)}, f32[160,1,1024]{2,1,0:T(1,128)S(1)}, u32[]{:S(2)}, u32[]{:S(2)}) collective-permute-start(f32[160,1,1024]{2,1,0:T(1,128)S(1)} %get-tuple-element.240), channel_id=1, source_target_pairs={{1,0},{2,1},{3,2},{4,3},{5,4},{6,5},{7,6},{8,7},{9,8},{10,9},{11,1... | collective-permute-start | bytes 1966088 | tf_op jit(solution)/shard_map/while/body/eval_jaxpr/ppermute | solution.py:22
  169.4 13.7 %collective-permute-start.3 = (f32[160,1,1024]{2,1,0:T(1,128)S(1)}, f32[160,1,1024]{2,1,0:T(1,128)}, u32[]{:S(2)}, u32[]{:S(2)}) collective-permute-start(f32[160,1,1024]{2,1,0:T(1,128)S(1)} %get-tuple-element.241), channel_id=1, source_target_pairs={{0,1},{1,2},{2,3},{3,4},{4,5},{5,6},{6,7},{7,8},{8,9},{9,10},{10,1... | collective-permute-start | bytes 1966088 | tf_op jit(solution)/shard_map/while/body/eval_jaxpr/ppermute | solution.py:20
  189.6 15.6 %copy-start.27 = (f32[4,1024]{1,0:T(4,128)S(1)}, f32[4,1024]{1,0:T(4,128)}, u32[]{:S(2)}) copy-start(f32[4,1024]{1,0:T(4,128)} %get-tuple-element.289) | copy-start | bytes 49156 | tf_op jit(solution)/shard_map/while
  189.6 16.2 %copy-start.25 = (f32[4,1024]{1,0:T(4,128)S(1)}, f32[4,1024]{1,0:T(4,128)}, u32[]{:S(2)}) copy-start(f32[4,1024]{1,0:T(4,128)} %get-tuple-element.288) | copy-start | bytes 49156 | tf_op jit(solution)/shard_map/while
  190.6 17.8 %collective-permute-start.2 = (f32[160,1,1024]{2,1,0:T(1,128)S(1)}, f32[160,1,1024]{2,1,0:T(1,128)S(1)}, u32[]{:S(2)}, u32[]{:S(2)}) collective-permute-start(f32[160,1,1024]{2,1,0:T(1,128)S(1)} %get-tuple-element.240), channel_id=1, source_target_pairs={{1,0},{2,1},{3,2},{4,3},{5,4},{6,5},{7,6},{8,7},{9,8},{10,9},{11,1... | collective-permute-start | bytes 1966088 | tf_op jit(solution)/shard_map/while/body/eval_jaxpr/ppermute | solution.py:22
  191.9 16.6 %collective-permute-start.3 = (f32[160,1,1024]{2,1,0:T(1,128)S(1)}, f32[160,1,1024]{2,1,0:T(1,128)}, u32[]{:S(2)}, u32[]{:S(2)}) collective-permute-start(f32[160,1,1024]{2,1,0:T(1,128)S(1)} %get-tuple-element.241), channel_id=1, source_target_pairs={{0,1},{1,2},{2,3},{3,4},{4,5},{5,6},{6,7},{7,8},{8,9},{9,10},{10,1... | collective-permute-start | bytes 1966088 | tf_op jit(solution)/shard_map/while/body/eval_jaxpr/ppermute | solution.py:20
  222.3 48.1 %copy-start.35 = (f32[6,2048]{1,0:T(8,128)S(1)}, f32[6,2048]{1,0:T(8,128)}, u32[]{:S(2)}) copy-start(f32[6,2048]{1,0:T(8,128)} %get-tuple-element.132) | copy-start | bytes 147460
  (82 other events, 436.9 us)
where the time goes:
time: 274 us; the launch traced here: 273 us
  starting transfers between devices  97.7 us (36%)
  local copies, waits for them, and re-layouts  59.1 us (22%)
  other arithmetic  50.8 us (19%)
  blocking collectives  45.8 us (17%)
  matrix products  17.2 us (6%)
    ppermute x9, starting transfers between devices, with_halo(): lax.ppermute(tail, axis, [(i, (i + 1) % count) for i in range(ends)])  86.1 us
    add x8, other arithmetic, transpose_step(): keep * centre + rate_n * padded[:, :-2] + rate_s * padded[:, 2:]  47.6 us
    psum x1, blocking collectives, month_total(): return lax.psum(local_grad, 'tile')  45.8 us
    slice x40, local copies, waits for them, and re-layouts, transpose_step(): r[begin:begin + count]  19.3 us
    slice x16, local copies, waits for them, and re-layouts, transpose_step(): jnp.roll(centre, 1, axis=2)  16.1 us
    ppermute x9, starting transfers between devices, with_halo(): lax.ppermute(head, axis, [((i + 1) % count, i) for i in range(ends)])  11.6 us
    slice x8, local copies, waits for them, and re-layouts, with_halo(): lax.slice_in_dim(cells, cells.shape[dim] - width, cells.shape[dim], axis=...  8.1 us
    unnamed x55, local copies, waits for them, and re-layouts  7.25 us
  transfers between devices with their start and end apart: 18, of which 0 were waited for; matrix products, arithmetic and copies ran while one was open for 16% of the time, Pallas kernels for 0%

commit v1 on v0

v1 whole, which is shorter than its diff:
```python
import jax
import jax.numpy as jnp
from jax import lax
from jax.experimental import pallas as pl
from jax.experimental.pallas import tpu as pltpu
from jax.sharding import PartitionSpec as P

SUBSTEPS = 4
LANES = 128
MESH = pl.DeviceIdType.MESH


def cuts(total, parts):
    size = max(1, total // parts)
    starts = [i * size for i in range(parts)]
    return [(s, (size if i < parts - 1 else total - s)) for i, s in enumerate(starts)]


def kernel(
    dims,
    pref,
    base,
    lead,
    dens1,
    dens2,
    food,
    fields,
    out,
    sens,
    grad,
    wide2,
    wide1,
    done2,
    done1,
    aged2,
    aged1,
    strip,
    rates,
    short_all,
    adem_all,
    short1,
    feed_sq,
    surv,
    lsend,
    lrecv,
    zsend,
    zrecv,
    osend,
    orecv,
    z1send,
    z1recv,
    o1send,
    o1recv,
    fsend,
    frecv,
    hsend,
    hrecv,
    ssend,
    srecv,
    asend,
    arecv,
    own_sem,
):
    tiles, group, cohorts, quarter, forage, chunks = dims
    half = group // 2
    blocks = food.shape[2]
    me = lax.axis_index("tile")
    q = lax.rem(me, group)
    first = me - q
    has_prev = me >= group
    has_next = me < tiles - group

    def peer(o):
        return first + lax.rem(q + o, group)

    def source(o):
        return lax.rem(q + group - o, group)

    barrier = pltpu.get_barrier_semaphore()
    for o in range(1, group):
        pl.semaphore_signal(barrier, inc=1, device_id={"tile": peer(o)}, device_id_type=MESH)

    @pl.when(has_prev)
    def _():
        pl.semaphore_signal(barrier, inc=1, device_id={"tile": me - group}, device_id_type=MESH)

    @pl.when(has_next)
    def _():
        pl.semaphore_signal(barrier, inc=1, device_id={"tile": me + group}, device_id_type=MESH)

    sides = has_prev.astype(jnp.int32) + has_next.astype(jnp.int32)
    pl.semaphore_wait(barrier, group - 1 + sides)

    def remote(src, dst, ssem, rsem, target):
        return pltpu.make_async_remote_copy(
            src_ref=src, dst_ref=dst, send_sem=ssem, recv_sem=rsem,
            device_id={"tile": target}, device_id_type=MESH,
        )

    def gather_copy(buf, ssem, rsem, o):
        return remote(buf.at[q], buf.at[q], ssem.at[o], rsem.at[o], peer(o))

    def gather_wait(buf, ssem, rsem, o):
        spot = buf.at[source(o)]
        remote(spot, spot, ssem.at[o], rsem.at[o], peer(o)).wait_recv()

    def halo(buf, lo, size, ssem, rsem, c):
        down = remote(
            buf.at[pl.ds(group, half), pl.ds(lo, size)], buf.at[pl.ds(0, half), pl.ds(lo, size)],
            ssem.at[0, c], rsem.at[0, c], me + group,
        )
        up = remote(
            buf.at[pl.ds(half, half), pl.ds(lo, size)],
            buf.at[pl.ds(group + half, half), pl.ds(lo, size)],
            ssem.at[1, c], rsem.at[1, c], me - group,
        )
        return down, up

    def halo_start(*args):
        down, up = halo(*args)

        @pl.when(has_next)
        def _():
            down.start()

        @pl.when(has_prev)
        def _():
            up.start()

    def halo_wait(*args):
        down, up = halo(*args)

        @pl.when(has_prev)
        def _():
            down.wait_recv()

        @pl.when(has_next)
        def _():
            up.wait_recv()

    def halo_sent(*args):
        down, up = halo(*args)

        @pl.when(has_next)
        def _():
            down.wait_send()

        @pl.when(has_prev)
        def _():
            up.wait_send()

    own_field = pltpu.make_async_copy(fields, strip.at[half + q], own_sem.at[0])
    own_field.start()
    for o in range(1, group):
        remote(fields, strip.at[half + q], fsend.at[o], frecv.at[o], peer(o)).start()

    lead_cuts = cuts(quarter + 1, chunks)
    part_cuts = cuts(quarter, chunks)

    def lead_copy(o, c):
        lo, size = lead_cuts[c]
        to = lax.rem(q + o, group)
        return remote(
            lead.at[pl.ds(to * quarter + lo, size)], wide2.at[half + q, pl.ds(lo, size)],
            lsend.at[o, c], lrecv.at[o, c], peer(o),
        )

    own_lead = pltpu.make_async_copy(
        lead.at[pl.ds(q * quarter, quarter + 1)], wide2.at[half + q], own_sem.at[1]
    )
    own_lead.start()
    for c in range(chunks):
        for o in range(1, group):
            lead_copy(o, c).start()

    @pl.when(jnp.logical_not(has_prev))
    def _():
        strip[0:half] = jnp.zeros((half,) + strip.shape[1:], jnp.float32)
        wide2[0:half] = jnp.zeros((half,) + wide2.shape[1:], jnp.float32)
        wide1[0:half] = jnp.zeros((half,) + wide1.shape[1:], jnp.float32)

    @pl.when(jnp.logical_not(has_next))
    def _():
        strip[group + half :] = jnp.zeros((half,) + strip.shape[1:], jnp.float32)
        wide2[group + half :] = jnp.zeros((half,) + wide2.shape[1:], jnp.float32)
        wide1[group + half :] = jnp.zeros((half,) + wide1.shape[1:], jnp.float32)

    zero = jnp.zeros((blocks, LANES), jnp.float32)

    def demands(dens):
        def step(a, sums):
            n = dens[a]
            return tuple(sums[k] + pref[a * forage + k] * n for k in range(forage))

        return lax.fori_loop(0, cohorts, step, (zero,) * forage, unroll=4)

    def prepare(month, dens, short_store):
        sums = demands(dens)
        for k in range(forage):
            feed = food[month, k]
            total = feed + sums[k]
            short_store(k, sums[k] / total)
            feed_sq[month, k] = feed / (total * total)
            feed_sq[2 + month, k] = sums[k]

    def store_two(k, value):
        short_all[q, k] = value

    def store_one(k, value):
        short1[k] = value

    prepare(1, dens2, store_two)
    for o in range(1, group):
        gather_copy(short_all, ssend, srecv, o).start()

    own_field.wait()
    for o in range(1, group):
        spot = strip.at[half + source(o)]
        remote(spot, spot, fsend.at[o], frecv.at[o], peer(o)).wait_recv()
    halo_start(strip, 0, 3, hsend, hrecv, 0)
    own_lead.wait()
    lane = lax.broadcasted_iota(jnp.int32, (blocks, LANES), 1)
    odd = lax.rem(lax.broadcasted_iota(jnp.int32, (blocks, LANES), 0), 2) == 1
    last_lane = lane == LANES - 1
    first_lane = lane == 0

    def east_of(x):
        near = pltpu.roll(x, LANES - 1, 1)
        return jnp.where(last_lane, pltpu.roll(near, blocks - 2, 0), near)

    def west_of(x):
        near = pltpu.roll(x, 1, 1)
        return jnp.where(first_lane, pltpu.roll(near, 2, 0), near)

    def vertical(slots, s):
        above = slots[s - 1] if s > 0 and slots[s - 1] is not None else zero
        below = slots[s + 1] if s + 1 < len(slots) and slots[s + 1] is not None else zero
        north = jnp.where(odd, pltpu.roll(slots[s], 1, 0), pltpu.roll(above, blocks - 1, 0))
        south = jnp.where(odd, pltpu.roll(below, 1, 0), pltpu.roll(slots[s], blocks - 1, 0))
        return north, south

    prepare(0, dens1, store_one)

    def lead_wait(c):
        lo, size = lead_cuts[c]
        for o in range(1, group):
            spot = wide2.at[half + source(o), pl.ds(lo, size)]
            remote(spot, spot, lsend.at[o, c], lrecv.at[o, c], peer(o)).wait_recv()

    lead_wait(0)
    halo_start(wide2, *lead_cuts[0], zsend, zrecv, 0)
    halo_wait(strip, 0, 3, hsend, hrecv, 0)
    masks = [strip[s, 0] for s in range(2 * group)]
    for s in range(2 * group):
        mask, east, north = masks[s], strip[s, 1], strip[s, 2]
        mask_n, mask_s = vertical(masks, s)
        rate_n = mask * mask_n * (0.1 + jnp.maximum(north, 0.0))
        rate_s = mask * mask_s * (0.1 + jnp.maximum(-north, 0.0))
        rate_e = mask * east_of(mask) * (0.1 + jnp.maximum(east, 0.0))
        rate_w = mask * west_of(mask) * (0.1 + jnp.maximum(-east, 0.0))
        rates[s, 0] = 1.0 - rate_n - rate_s - rate_e - rate_w
        rates[s, 1] = rate_n
        rates[s, 2] = rate_s
        rates[s, 3] = rate_e
        rates[s, 4] = rate_w

    def transport(wide, done, lo, size):
        def body(i, carry):
            slots = [wide[s, i] for s in range(2 * group)]
            for step in range(SUBSTEPS):
                margin = (step + 1) // 2
                new = [None] * (2 * group)
                for s in range(margin, 2 * group - margin):
                    north, south = vertical(slots, s)
                    new[s] = (
                        rates[s, 0] * slots[s]
                        + rates[s, 1] * north
                        + rates[s, 2] * south
                        + rates[s, 3] * east_of(slots[s])
                        + rates[s, 4] * west_of(slots[s])
                    )
                slots = new
            for s in range(group):
                done[s, i] = slots[half + s]
            return carry

        lax.fori_loop(lo, lo + size, body, 0)

    def out_copy(done, aged, o, c, ssem, rsem):
        lo, size = part_cuts[c]
        return remote(
            done.at[lax.rem(q + o, group), pl.ds(lo, size)],
            aged.at[pl.ds(q * quarter + lo, size)], ssem.at[o, c], rsem.at[o, c], peer(o),
        )

    def out_own(done, aged, c, sem):
        lo, size = part_cuts[c]
        return pltpu.make_async_copy(
            done.at[q, pl.ds(lo, size)], aged.at[pl.ds(q * quarter + lo, size)], sem.at[0, c]
        )

    def out_wait(aged, o, c, ssem, rsem):
        lo, size = part_cuts[c]
        spot = aged.at[pl.ds(source(o) * quarter + lo, size)]
        remote(spot, spot, ssem.at[o, c], rsem.at[o, c], peer(o)).wait_recv()

    for c in range(chunks):
        if c + 1 < chunks:
            lead_wait(c + 1)
            halo_start(wide2, *lead_cuts[c + 1], zsend, zrecv, c + 1)
        halo_wait(wide2, *lead_cuts[c], zsend, zrecv, c)
        transport(wide2, done2, *lead_cuts[c])
        for o in range(1, group):
            out_copy(done2, aged2, o, c, osend, orecv).start()
        out_own(done2, aged2, c, orecv).start()

    def ratio_part(lo, size, aged, dens, short, sums):
        def step(a, sums):
            level = base[a]
            hunger = [pref[a * forage + k] for k in range(forage)]
            for k in range(forage):
                level = level + hunger[k] * short[k]
            kept = jnp.exp(-level)
            surv[a] = kept
            dying = aged[a] * kept * dens[a]
            return tuple(sums[k] + hunger[k] * dying for k in range(forage))

        for part in range(group):
            start = part * quarter + lo
            sums = lax.fori_loop(start, start + size, step, sums, unroll=2)
        return sums

    def finish(month, ratio):
        adem = []
        for k in range(forage):
            adem.append(-ratio[k] * feed_sq[month, k])
            sens[month, k] = ratio[k] * feed_sq[2 + month, k] * feed_sq[month, k]
        return adem

    def slopes(aged, dens, short, adem, add):
        def step(a, carry):
            n = dens[a]
            kept = surv[a]
            dying = aged[a] * kept * n
            rows = []
            for k in range(forage):
                both = n * adem[k] - dying * short[k]
                rows.append(jnp.sum(both, axis=0, keepdims=True))
            rows = jnp.concatenate(rows, axis=0)
            if add:
                rows = rows + grad[a]
                total = aged[a] * kept
                for k in range(forage):
                    total = total + pref[a * forage + k] * adem[k]
                out[a] = total
            grad[a] = rows
            return carry

        lax.fori_loop(0, cohorts, step, 0, unroll=2)

    short2 = [short_all[q, k] for k in range(forage)]
    ratio = (zero,) * forage
    for c in range(chunks):
        for o in range(1, group):
            out_wait(aged2, o, c, osend, orecv)
        out_own(done2, aged2, c, orecv).wait()
        ratio = ratio_part(*part_cuts[c], aged2, dens2, short2, ratio)
    adem2 = finish(1, ratio)
    for k in range(forage):
        adem_all[q, k] = adem2[k]
    for o in range(1, group):
        gather_copy(adem_all, asend, arecv, o).start()
    for o in range(1, group):
        gather_wait(short_all, ssend, srecv, o)
    for o in range(1, group):
        gather_wait(adem_all, asend, arecv, o)

    for c in range(chunks):
        lo, size = part_cuts[c]

        def middle(i, carry):
            a = jnp.minimum(q * quarter + i + 1, cohorts - 1)
            hunger = [pref[a * forage + k] for k in range(forage)]
            for s in range(group):
                level = base[a]
                add = zero
                for k in range(forage):
                    level = level + hunger[k] * short_all[s, k]
                    add = add + hunger[k] * adem_all[s, k]
                wide1[half + s, i] = done2[s, i + 1] * jnp.exp(-level) + add
            return carry

        lax.fori_loop(lo, lo + size, middle, 0)
        halo_start(wide1, lo, size, z1send, z1recv, c)
    slopes(aged2, dens2, short2, adem2, False)

    for c in range(chunks):
        halo_wait(wide1, *part_cuts[c], z1send, z1recv, c)
        transport(wide1, done1, *part_cuts[c])
        for o in range(1, group):
            out_copy(done1, aged1, o, c, o1send, o1recv).start()
        out_own(done1, aged1, c, o1recv).start()

    short_one = [short1[k] for k in range(forage)]
    ratio = (zero,) * forage
    for c in range(chunks):
        for o in range(1, group):
            out_wait(aged1, o, c, o1send, o1recv)
        out_own(done1, aged1, c, o1recv).wait()
        ratio = ratio_part(*part_cuts[c], aged1, dens1, short_one, ratio)
    adem1 = finish(0, ratio)
    slopes(aged1, dens1, short_one, adem1, True)

    for o in range(1, group):
        remote(fields, strip.at[half + q], fsend.at[o], frecv.at[o], peer(o)).wait_send()
        gather_copy(short_all, ssend, srecv, o).wait_send()
        gather_copy(adem_all, asend, arecv, o).wait_send()
        for c in range(chunks):
            lead_copy(o, c).wait_send()
            out_copy(done2, aged2, o, c, osend, orecv).wait_send()
            out_copy(done1, aged1, o, c, o1send, o1recv).wait_send()
    halo_sent(strip, 0, 3, hsend, hrecv, 0)
    for c in range(chunks):
        halo_sent(wide2, *lead_cuts[c], zsend, zrecv, c)
        halo_sent(wide1, *part_cuts[c], z1send, z1recv, c)


def blocked(x):
    rows, columns = x.shape[-2:]
    head = x.shape[:-2]
    n = len(head)
    y = x.reshape(head + (rows, columns // LANES, LANES))
    y = jnp.swapaxes(y, n, n + 1)
    return y.reshape(head + (rows * columns // LANES, LANES))


def unblocked(x, rows):
    head = x.shape[:-2]
    n = len(head)
    y = x.reshape(head + (x.shape[-2] // rows, rows, LANES))
    y = jnp.swapaxes(y, n, n + 1)
    return y.reshape(head + (rows, -1))


def shards(
    final_adjoint,
    first_density,
    second_density,
    forage,
    preference,
    base_mortality,
    age_class,
    land_mask,
    east_velocity,
    north_velocity,
):
    classes, groups = preference.shape
    cohorts, rows, columns = final_adjoint.shape
    tiles = lax.axis_size("tile")
    group = 2 * SUBSTEPS // rows
    quarter = cohorts // group
    chunks = 5
    blocks = rows * columns // LANES
    pref_rows = preference[age_class]
    fields = blocked(jnp.stack([land_mask.astype(jnp.float32), east_velocity, north_velocity]))
    incoming = blocked(final_adjoint)
    tail = incoming[cohorts - 1 :]
    lead = jnp.concatenate([incoming[1:], tail, tail], axis=0)
    f32 = jnp.float32
    dma = pltpu.SemaphoreType.DMA
    vmem = pl.BlockSpec(memory_space=pltpu.VMEM)
    smem = pl.BlockSpec(memory_space=pltpu.SMEM)
    dims = (tiles, group, cohorts, quarter, groups, chunks)
    cell = (blocks, LANES)
    pair = [dma((group, chunks)), dma((group, chunks))]
    hop = [dma((2, chunks)), dma((2, chunks))]
    one = [dma((group,)), dma((group,))]

    def body(*refs):
        kernel(dims, *refs)

    out, sens, grad = pl.pallas_call(
        body,
        out_shape=(
            jax.ShapeDtypeStruct((cohorts,) + cell, f32),
            jax.ShapeDtypeStruct((2, groups) + cell, f32),
            jax.ShapeDtypeStruct((cohorts, groups, LANES), f32),
        ),
        in_specs=[smem, smem] + [vmem] * 5,
        out_specs=(vmem, vmem, vmem),
        scratch_shapes=[
            pltpu.VMEM((2 * group, quarter + 1) + cell, f32),
            pltpu.VMEM((2 * group, quarter) + cell, f32),
            pltpu.VMEM((group, quarter + 1) + cell, f32),
            pltpu.VMEM((group, quarter) + cell, f32),
            pltpu.VMEM((cohorts,) + cell, f32),
            pltpu.VMEM((cohorts,) + cell, f32),
            pltpu.VMEM((2 * group, 3) + cell, f32),
            pltpu.VMEM((2 * group, 5) + cell, f32),
            pltpu.VMEM((group, groups) + cell, f32),
            pltpu.VMEM((group, groups) + cell, f32),
            pltpu.VMEM((groups,) + cell, f32),
            pltpu.VMEM((4, groups) + cell, f32),
            pltpu.VMEM((cohorts,) + cell, f32),
        ]
        + pair + hop + pair + hop + pair + one
        + [dma((2, 1)), dma((2, 1))] + one + one + [dma((2,))],
        compiler_params=pltpu.CompilerParams(
            collective_id=0, has_side_effects=True, vmem_limit_bytes=48 * 1024 * 1024
        ),
        name="adjoint",
    )(
        pref_rows.reshape(-1),
        base_mortality,
        lead,
        blocked(first_density),
        blocked(second_density),
        blocked(forage),
        fields,
    )
    onehot = (age_class[None, :] == jnp.arange(classes, dtype=jnp.int32)[:, None]).astype(f32)
    local = jnp.dot(onehot, jnp.sum(grad, axis=2), precision=lax.Precision.HIGHEST)
    cells = land_mask.shape[0] * tiles * land_mask.shape[1]
    summed = lax.psum(local, "tile") / cells
    return (unblocked(out, rows), unblocked(sens, rows), summed)


def solution(mesh):
    in_specs = (
        P("ens", "tile", None),
        P("ens", "tile", None),
        P("ens", "tile", None),
        P("ens", None, "tile", None),
        P("ens", None),
        P(),
        P(),
        P("tile", None),
        P("tile", None),
        P("tile", None),
    )
    out_specs = (P("ens", "tile", None), P("ens", None, "tile", None), P("ens", None))
    return jax.shard_map(shards, mesh=mesh, in_specs=in_specs, out_specs=out_specs, check_vma=False)
```

time: 274 us -> 115 us (0.42)
  starting transfers between devices: 97.7 us -> 0 us
  Pallas kernels: 0 us -> 70.4 us
  local copies, waits for them, and re-layouts: 59.1 us -> 7.35 us
  other arithmetic: 50.8 us -> 3.05 us
  matrix products: 17.2 us -> 0.22 us
  blocking collectives: 45.8 us -> 32.7 us
    ppermute x18 -> x0, starting transfers between devices: 97.7 us -> none  [the longest x9 86.1 us: with_halo(): lax.ppermute(tail, axis, [(i, (i + 1) % count) for i in range(ends)])]
    pallas_call x0 -> x1, Pallas kernels: none -> 70.4 us  [shards(): pl.pallas_call(body, out_shape=(jax.ShapeDtypeStruct((cohorts,) + cell, f...]
    add x8 -> x0, other arithmetic: 47.6 us -> none  [transpose_step(): keep * centre + rate_n * padded[:, :-2] + rate_s * padded[:, 2:]]
    slice x70 -> x2, local copies, waits for them, and re-layouts: 44.5 us -> 2.49 us  [the longest x1 1.8 us: shards(): lead = jnp.concatenate([incoming[1:], tail, tail], axis=0)]
    dot_general x15 -> x1, matrix products: 17.2 us -> 0.22 us  [shards(): jnp.dot(onehot, jnp.sum(grad, axis=2), precision=lax.Precision.HIGHEST)]
    psum x1, blocking collectives: 45.8 us -> 32.7 us  [shards(): summed = lax.psum(local, 'tile') / cells]
    while x152 -> x0, local copies, waits for them, and re-layouts: 3.91 us -> none
    unnamed x55 -> x13, local copies, waits for them, and re-layouts: 7.25 us -> 4.06 us
  transfers between devices with their start and end apart: 18 -> 0, of which waited for: 0 -> 0; matrix products, arithmetic and copies ran while one was open for 16% -> 0% of each run, Pallas kernels for 0% -> 0%
where the time goes in v1:
time: 115 us; the launch traced here: 114 us
  Pallas kernels  70.4 us (61%)
  blocking collectives  32.7 us (28%)
  local copies, waits for them, and re-layouts  7.35 us (6%)
  other arithmetic  3.05 us (3%)
    pallas_call x1, Pallas kernels, shards(): pl.pallas_call(body, out_shape=(jax.ShapeDtypeStruct((cohorts,) + cell, f...  70.4 us
    psum x1, blocking collectives, shards(): summed = lax.psum(local, 'tile') / cells  32.7 us
    unnamed x13, local copies, waits for them, and re-layouts  4.06 us

profile of v1, /device:TPU:0, one launch (start us, length us, event | category | flops | bytes accessed | tf_op | source)
XLA Modules:
  0.0 114.4 jit_solution(6501587695853588124)
XLA Ops:
  0.6 0.7 compare_select_fusion
  1.3 0.7 slice.19
  2.0 0.8 copy.23
  2.8 0.7 convert_bitcast_fusion
  3.5 0.7 pad_maximum_fusion.1
  4.2 0.7 gather_fusion
  4.9 0.1 reshape.56.refs_0_
  5.0 0.0 copy-start.2
  5.0 1.8 %slice.18 = f32[159,8,2,128]{3,2,1,0:T(2,128)S(1)} slice(f32[160,8,2,128]{3,2,1,0:T(2,128)} %bitcast.46), slice={[1:160], [0:8], [0:2], [0:128]} | slice | bytes 2605056 | tf_op jit(solution)/shard_map/slice | solution.py:468
  6.8 0.0 copy-start
  6.9 0.0 copy-start.1
  6.9 0.0 copy-start.3
  6.9 0.1 pad_maximum_fusion.refs_2_
  7.0 0.0 copy-done.2
  7.0 1.2 %copy-done = f32[160,2,1024]{2,1,0:T(2,128)S(1)} copy-done((f32[160,2,1024]{2,1,0:T(2,128)S(1)}, f32[160,2,1024]{2,1,0:T(2,128)}, u32[]{:S(2)}) %copy-start) | copy-done | bytes 1310744
  8.2 0.4 copy-done.1
  8.6 0.0 copy-done.3
  8.6 0.0 copy-start.4
  8.6 70.4 %adjoint.1 = (f32[160,16,128]{2,1,0:T(8,128)S(1)}, f32[2,6,16,128]{3,2,1,0:T(8,128)S(1)}, f32[160,6,128]{2,1,0:T(8,128)S(1)}) custom-call(f32[960]{0:T(1024)S(1)} %reshape.56.refs_0_, f32[160]{0:T(256)S(1)} %copy-done.3, f32[161,16,128]{2,1,0:T(8,128)S(1)} %pad_maximum_fusion.refs_2_, f32[160,16,128]{2,1,0:T(8,128)S(1)} %bitcast.39, ...), custom_call_target="tpu_custom_call" | custom-call | tf_op jit(solution)/shard_map/adjoint/pallas_call | solution.py:482
  79.0 0.2 reduce_sum.9
  79.2 0.0 copy-done.4
  79.2 0.2 fusion
  79.5 32.7 %psum.7 = f32[16,6]{0,1:T(8,128)S(1)} all-reduce(f32[16,6]{0,1:T(8,128)S(1)} %fusion), channel_id=1, replica_groups=mesh['ens'=2,'tile'=16] {'tile'}, use_global_device_ids=true, to_apply=%region_1.0 | all-reduce | flops 96 | bytes 768 | tf_op jit(solution)/shard_map/psum | solution.py:524
  112.1 0.6 broadcast_multiply_fusion
  112.7 1.1 copy.35
  113.8 0.6 copy.36
  (1 shorter events, 0.0 us)
Async XLA Ops:
  5.0 1.9 %copy-start.2 = (f32[2,6,2,1024]{3,2,1,0:T(2,128)S(1)}, f32[2,6,2,1024]{3,2,1,0:T(2,128)}, u32[]{:S(2)}) copy-start(f32[2,6,2,1024]{3,2,1,0:T(2,128)} %param.13) | copy-start | bytes 294916
  6.8 1.3 %copy-start = (f32[160,2,1024]{2,1,0:T(2,128)S(1)}, f32[160,2,1024]{2,1,0:T(2,128)}, u32[]{:S(2)}) copy-start(f32[160,2,1024]{2,1,0:T(2,128)} %param.11) | copy-start | bytes 3932164
  6.9 1.7 %copy-start.1 = (f32[160,2,1024]{2,1,0:T(2,128)S(1)}, f32[160,2,1024]{2,1,0:T(2,128)}, u32[]{:S(2)}) copy-start(f32[160,2,1024]{2,1,0:T(2,128)} %param.12) | copy-start | bytes 3932164
  6.9 1.7 %copy-start.3 = (f32[160]{0:T(256)S(1)}, f32[160]{0:T(256)}, u32[]{:S(2)}) copy-start(f32[160]{0:T(256)} %refs_1_.1) | copy-start | bytes 1924
  8.6 70.7 %copy-start.4 = (s32[160]{0:T(256)S(1)}, s32[160]{0:T(256)}, u32[]{:S(2)}) copy-start(s32[160]{0:T(256)} %param.16) | copy-start | bytes 1924

commit v2 on v1

--- a/solution.py
+++ b/solution.py
@@ -18,29 +18,38 @@
 
 def kernel(
     dims,
-    pref,
+    table,
     base,
+    cls,
     lead,
     dens1,
     dens2,
     food,
-    fields,
+    mask_in,
+    east_in,
+    north_in,
+    cls_row,
     out,
     sens,
-    grad,
+    grad_out,
     wide2,
     wide1,
     done2,
     done1,
     aged2,
     aged1,
-    strip,
+    mask_strip,
+    east_strip,
+    north_strip,
     rates,
     short_all,
     adem_all,
     short1,
     feed_sq,
     surv,
+    grad,
+    near_sum,
+    far_sum,
     lsend,
     lrecv,
     zsend,
@@ -59,6 +68,10 @@
     srecv,
     asend,
     arecv,
+    nsend,
+    nrecv,
+    tsend,
+    trecv,
     own_sem,
 ):
     tiles, group, cohorts, quarter, forage, chunks = dims
@@ -80,16 +93,14 @@
     for o in range(1, group):
         pl.semaphore_signal(barrier, inc=1, device_id={"tile": peer(o)}, device_id_type=MESH)
 
-    @pl.when(has_prev)
-    def _():
-        pl.semaphore_signal(barrier, inc=1, device_id={"tile": me - group}, device_id_type=MESH)
-
-    @pl.when(has_next)
-    def _():
-        pl.semaphore_signal(barrier, inc=1, device_id={"tile": me + group}, device_id_type=MESH)
-
-    sides = has_prev.astype(jnp.int32) + has_next.astype(jnp.int32)
-    pl.semaphore_wait(barrier, group - 1 + sides)
+    spans = tiles // group
+    for g in range(1, spans):
+        far = lax.rem(me + g * group, tiles)
+        pl.semaphore_signal(barrier, inc=1, device_id={"tile": far}, device_id_type=MESH)
+    pl.semaphore_wait(barrier, group + spans - 2)
+
+    def pref(a, k):
+        return table[cls[a], k]
 
     def remote(src, dst, ssem, rsem, target):
         return pltpu.make_async_remote_copy(
@@ -105,15 +116,13 @@
         remote(spot, spot, ssem.at[o], rsem.at[o], peer(o)).wait_recv()
 
     def halo(buf, lo, size, ssem, rsem, c):
-        down = remote(
-            buf.at[pl.ds(group, half), pl.ds(lo, size)], buf.at[pl.ds(0, half), pl.ds(lo, size)],
-            ssem.at[0, c], rsem.at[0, c], me + group,
-        )
-        up = remote(
-            buf.at[pl.ds(half, half), pl.ds(lo, size)],
-            buf.at[pl.ds(group + half, half), pl.ds(lo, size)],
-            ssem.at[1, c], rsem.at[1, c], me - group,
-        )
+        def rows(begin):
+            if lo is None:
+                return buf.at[pl.ds(begin, half)]
+            return buf.at[pl.ds(begin, half), pl.ds(lo, size)]
+
+        down = remote(rows(group), rows(0), ssem.at[0, c], rsem.at[0, c], me + group)
+        up = remote(rows(half), rows(group + half), ssem.at[1, c], rsem.at[1, c], me - group)
         return down, up
 
     def halo_start(*args):
@@ -149,39 +158,61 @@
         def _():
             up.wait_send()
 
-    own_field = pltpu.make_async_copy(fields, strip.at[half + q], own_sem.at[0])
-    own_field.start()
-    for o in range(1, group):
-        remote(fields, strip.at[half + q], fsend.at[o], frecv.at[o], peer(o)).start()
+    strips = ((mask_in, mask_strip), (east_in, east_strip), (north_in, north_strip))
+    own_fields = [
+        pltpu.make_async_copy(src, dst.at[half + q], own_sem.at[f])
+        for f, (src, dst) in enumerate(strips)
+    ]
+    for copy in own_fields:
+        copy.start()
+
+    def field_copy(o, f):
+        src, dst = strips[f]
+        return remote(src, dst.at[half + q], fsend.at[o, f], frecv.at[o, f], peer(o))
+
+    for f in range(3):
+        for o in range(1, group):
+            field_copy(o, f).start()
 
     lead_cuts = cuts(quarter + 1, chunks)
     part_cuts = cuts(quarter, chunks)
-
-    def lead_copy(o, c):
-        lo, size = lead_cuts[c]
-        to = lax.rem(q + o, group)
+    tail = lead_cuts[-1][0]
+    lead_parts = lead_cuts[:-1] + [(tail, quarter - 1 - tail), (quarter - 1, 1), (quarter, 1)]
+
+    def lead_copy(o, p):
+        lo, size = lead_parts[p]
+        begin = lax.rem(q + o, group) * quarter + 1 + lo
         return remote(
-            lead.at[pl.ds(to * quarter + lo, size)], wide2.at[half + q, pl.ds(lo, size)],
-            lsend.at[o, c], lrecv.at[o, c], peer(o),
+            lead.at[pl.ds(jnp.minimum(begin, cohorts - size), size)],
+            wide2.at[half + q, pl.ds(lo, size)],
+            lsend.at[o, p], lrecv.at[o, p], peer(o),
         )
 
-    own_lead = pltpu.make_async_copy(
-        lead.at[pl.ds(q * quarter, quarter + 1)], wide2.at[half + q], own_sem.at[1]
-    )
-    own_lead.start()
-    for c in range(chunks):
+    def lead_own(p):
+        lo, size = lead_parts[p]
+        begin = jnp.minimum(q * quarter + 1 + lo, cohorts - size)
+        return pltpu.make_async_copy(
+            lead.at[pl.ds(begin, size)], wide2.at[half + q, pl.ds(lo, size)], lrecv.at[0, p]
+        )
+
+    for p in range(len(lead_parts)):
         for o in range(1, group):
-            lead_copy(o, c).start()
+            lead_copy(o, p).start()
+        lead_own(p).start()
 
     @pl.when(jnp.logical_not(has_prev))
     def _():
-        strip[0:half] = jnp.zeros((half,) + strip.shape[1:], jnp.float32)
+        mask_strip[0:half] = jnp.zeros((half,) + mask_strip.shape[1:], jnp.int32)
+        east_strip[0:half] = jnp.zeros((half,) + east_strip.shape[1:], jnp.float32)
+        north_strip[0:half] = jnp.zeros((half,) + east_strip.shape[1:], jnp.float32)
         wide2[0:half] = jnp.zeros((half,) + wide2.shape[1:], jnp.float32)
         wide1[0:half] = jnp.zeros((half,) + wide1.shape[1:], jnp.float32)
 
     @pl.when(jnp.logical_not(has_next))
     def _():
-        strip[group + half :] = jnp.zeros((half,) + strip.shape[1:], jnp.float32)
+        mask_strip[group + half :] = jnp.zeros((half,) + mask_strip.shape[1:], jnp.int32)
+        east_strip[group + half :] = jnp.zeros((half,) + east_strip.shape[1:], jnp.float32)
+        north_strip[group + half :] = jnp.zeros((half,) + east_strip.shape[1:], jnp.float32)
         wide2[group + half :] = jnp.zeros((half,) + wide2.shape[1:], jnp.float32)
         wide1[group + half :] = jnp.zeros((half,) + wide1.shape[1:], jnp.float32)
 
@@ -190,7 +221,7 @@
     def demands(dens):
         def step(a, sums):
             n = dens[a]
-            return tuple(sums[k] + pref[a * forage + k] * n for k in range(forage))
+            return tuple(sums[k] + pref(a, k) * n for k in range(forage))
 
         return lax.fori_loop(0, cohorts, step, (zero,) * forage, unroll=4)
 
@@ -213,12 +244,12 @@
     for o in range(1, group):
         gather_copy(short_all, ssend, srecv, o).start()
 
-    own_field.wait()
-    for o in range(1, group):
-        spot = strip.at[half + source(o)]
-        remote(spot, spot, fsend.at[o], frecv.at[o], peer(o)).wait_recv()
-    halo_start(strip, 0, 3, hsend, hrecv, 0)
-    own_lead.wait()
+    for f, (src, dst) in enumerate(strips):
+        own_fields[f].wait()
+        for o in range(1, group):
+            spot = dst.at[half + source(o)]
+            remote(spot, spot, fsend.at[o, f], frecv.at[o, f], peer(o)).wait_recv()
+        halo_start(dst, None, None, hsend, hrecv, f)
     lane = lax.broadcasted_iota(jnp.int32, (blocks, LANES), 1)
     odd = lax.rem(lax.broadcasted_iota(jnp.int32, (blocks, LANES), 0), 2) == 1
     last_lane = lane == LANES - 1
@@ -242,17 +273,20 @@
     prepare(0, dens1, store_one)
 
     def lead_wait(c):
-        lo, size = lead_cuts[c]
-        for o in range(1, group):
-            spot = wide2.at[half + source(o), pl.ds(lo, size)]
-            remote(spot, spot, lsend.at[o, c], lrecv.at[o, c], peer(o)).wait_recv()
+        for p in [c] if c < chunks - 1 else range(c, len(lead_parts)):
+            lo, size = lead_parts[p]
+            for o in range(1, group):
+                spot = wide2.at[half + source(o), pl.ds(lo, size)]
+                remote(spot, spot, lsend.at[o, p], lrecv.at[o, p], peer(o)).wait_recv()
+            lead_own(p).wait()
 
     lead_wait(0)
     halo_start(wide2, *lead_cuts[0], zsend, zrecv, 0)
-    halo_wait(strip, 0, 3, hsend, hrecv, 0)
-    masks = [strip[s, 0] for s in range(2 * group)]
+    for f, (src, dst) in enumerate(strips):
+        halo_wait(dst, None, None, hsend, hrecv, f)
+    masks = [mask_strip[s].astype(jnp.float32) for s in range(2 * group)]
     for s in range(2 * group):
-        mask, east, north = masks[s], strip[s, 1], strip[s, 2]
+        mask, east, north = masks[s], east_strip[s], north_strip[s]
         mask_n, mask_s = vertical(masks, s)
         rate_n = mask * mask_n * (0.1 + jnp.maximum(north, 0.0))
         rate_s = mask * mask_s * (0.1 + jnp.maximum(-north, 0.0))
@@ -317,7 +351,7 @@
     def ratio_part(lo, size, aged, dens, short, sums):
         def step(a, sums):
             level = base[a]
-            hunger = [pref[a * forage + k] for k in range(forage)]
+            hunger = [pref(a, k) for k in range(forage)]
             for k in range(forage):
                 level = level + hunger[k] * short[k]
             kept = jnp.exp(-level)
@@ -340,23 +374,26 @@
     def slopes(aged, dens, short, adem, add):
         def step(a, carry):
             n = dens[a]
-            kept = surv[a]
-            dying = aged[a] * kept * n
-            rows = []
+            dying = aged[a] * surv[a] * n
             for k in range(forage):
                 both = n * adem[k] - dying * short[k]
-                rows.append(jnp.sum(both, axis=0, keepdims=True))
-            rows = jnp.concatenate(rows, axis=0)
-            if add:
-                rows = rows + grad[a]
-                total = aged[a] * kept
-                for k in range(forage):
-                    total = total + pref[a * forage + k] * adem[k]
-                out[a] = total
-            grad[a] = rows
+                row = jnp.sum(both, axis=0, keepdims=True)
+                if add:
+                    row = row + grad[k, pl.ds(a, 1)]
+                grad[k, pl.ds(a, 1)] = row
             return carry
 
         lax.fori_loop(0, cohorts, step, 0, unroll=2)
+
+    def outgoing(aged, adem):
+        def step(a, carry):
+            total = aged[a] * surv[a]
+            for k in range(forage):
+                total = total + pref(a, k) * adem[k]
+            out[a] = total
+            return carry
+
+        lax.fori_loop(0, cohorts, step, 0, unroll=4)
 
     short2 = [short_all[q, k] for k in range(forage)]
     ratio = (zero,) * forage
@@ -380,7 +417,7 @@
 
         def middle(i, carry):
             a = jnp.minimum(q * quarter + i + 1, cohorts - 1)
-            hunger = [pref[a * forage + k] for k in range(forage)]
+            hunger = [pref(a, k) for k in range(forage)]
             for s in range(group):
                 level = base[a]
                 add = zero
@@ -411,15 +448,58 @@
     adem1 = finish(0, ratio)
     slopes(aged1, dens1, short_one, adem1, True)
 
-    for o in range(1, group):
-        remote(fields, strip.at[half + q], fsend.at[o], frecv.at[o], peer(o)).wait_send()
+    classes = table.shape[0]
+    kinds = lax.broadcasted_iota(jnp.int32, (classes, cohorts), 0)
+    onehot = (kinds == cls_row[...]).astype(jnp.float32)
+    high = lax.Precision.HIGHEST
+    by_class = jnp.concatenate(
+        [
+            jnp.dot(onehot, grad[k], precision=high, preferred_element_type=jnp.float32)
+            for k in range(forage)
+        ],
+        axis=0,
+    )
+    ones = jnp.ones((8, LANES), jnp.float32)
+    near_sum[q] = lax.dot_general(
+        ones, by_class, (((1,), (1,)), ((), ())), precision=high,
+        preferred_element_type=jnp.float32,
+    )
+    for o in range(1, group):
+        gather_copy(near_sum, nsend, nrecv, o).start()
+    for o in range(1, group):
+        gather_wait(near_sum, nsend, nrecv, o)
+    span = me // group
+    far_sum[span] = sum(near_sum[i] for i in range(1, group)) + near_sum[0]
+
+    def far_copy(g):
+        far = lax.rem(me + g * group, tiles)
+        return remote(far_sum.at[span], far_sum.at[span], tsend.at[g], trecv.at[g], far)
+
+    for g in range(1, spans):
+        far_copy(g).start()
+    outgoing(aged1, adem1)
+    for g in range(1, spans):
+        spot = far_sum.at[lax.rem(span + spans - g, spans)]
+        remote(spot, spot, tsend.at[g], trecv.at[g], lax.rem(me + g * group, tiles)).wait_recv()
+    grad_out[...] = lax.fori_loop(
+        1, spans, lambda g, total: total + far_sum[g], far_sum[0]
+    ) / (tiles * blocks * LANES)
+    for g in range(1, spans):
+        far_copy(g).wait_send()
+
+    for o in range(1, group):
+        gather_copy(near_sum, nsend, nrecv, o).wait_send()
+        for f in range(3):
+            field_copy(o, f).wait_send()
+        for p in range(len(lead_parts)):
+            lead_copy(o, p).wait_send()
         gather_copy(short_all, ssend, srecv, o).wait_send()
         gather_copy(adem_all, asend, arecv, o).wait_send()
         for c in range(chunks):
-            lead_copy(o, c).wait_send()
             out_copy(done2, aged2, o, c, osend, orecv).wait_send()
             out_copy(done1, aged1, o, c, o1send, o1recv).wait_send()
-    halo_sent(strip, 0, 3, hsend, hrecv, 0)
+    for f, (src, dst) in enumerate(strips):
+        halo_sent(dst, None, None, hsend, hrecv, f)
     for c in range(chunks):
         halo_sent(wide2, *lead_cuts[c], zsend, zrecv, c)
         halo_sent(wide1, *part_cuts[c], z1send, z1recv, c)
@@ -461,15 +541,11 @@
     quarter = cohorts // group
     chunks = 5
     blocks = rows * columns // LANES
-    pref_rows = preference[age_class]
-    fields = blocked(jnp.stack([land_mask.astype(jnp.float32), east_velocity, north_velocity]))
-    incoming = blocked(final_adjoint)
-    tail = incoming[cohorts - 1 :]
-    lead = jnp.concatenate([incoming[1:], tail, tail], axis=0)
     f32 = jnp.float32
     dma = pltpu.SemaphoreType.DMA
     vmem = pl.BlockSpec(memory_space=pltpu.VMEM)
     smem = pl.BlockSpec(memory_space=pltpu.SMEM)
+    hbm = pl.BlockSpec(memory_space=pl.ANY)
     dims = (tiles, group, cohorts, quarter, groups, chunks)
     cell = (blocks, LANES)
     pair = [dma((group, chunks)), dma((group, chunks))]
@@ -484,9 +560,9 @@
         out_shape=(
             jax.ShapeDtypeStruct((cohorts,) + cell, f32),
             jax.ShapeDtypeStruct((2, groups) + cell, f32),
-            jax.ShapeDtypeStruct((cohorts, groups, LANES), f32),
+            jax.ShapeDtypeStruct((8, groups * classes), f32),
         ),
-        in_specs=[smem, smem] + [vmem] * 5,
+        in_specs=[smem, smem, smem, hbm] + [vmem] * 7,
         out_specs=(vmem, vmem, vmem),
         scratch_shapes=[
             pltpu.VMEM((2 * group, quarter + 1) + cell, f32),
@@ -495,33 +571,39 @@
             pltpu.VMEM((group, quarter) + cell, f32),
             pltpu.VMEM((cohorts,) + cell, f32),
             pltpu.VMEM((cohorts,) + cell, f32),
-            pltpu.VMEM((2 * group, 3) + cell, f32),
+            pltpu.VMEM((2 * group,) + cell, jnp.int32),
+            pltpu.VMEM((2 * group,) + cell, f32),
+            pltpu.VMEM((2 * group,) + cell, f32),
             pltpu.VMEM((2 * group, 5) + cell, f32),
             pltpu.VMEM((group, groups) + cell, f32),
             pltpu.VMEM((group, groups) + cell, f32),
             pltpu.VMEM((groups,) + cell, f32),
             pltpu.VMEM((4, groups) + cell, f32),
             pltpu.VMEM((cohorts,) + cell, f32),
+            pltpu.VMEM((groups, cohorts, LANES), f32),
+            pltpu.VMEM((group, 8, groups * classes), f32),
+            pltpu.VMEM((tiles // group, 8, groups * classes), f32),
         ]
-        + pair + hop + pair + hop + pair + one
-        + [dma((2, 1)), dma((2, 1))] + one + one + [dma((2,))],
+        + [dma((group, chunks + 2))] * 2 + hop + pair + hop + pair + [dma((group, 3))] * 2
+        + [dma((2, 3))] * 2 + one + one + one + [dma((tiles // group,))] * 2 + [dma((3,))],
         compiler_params=pltpu.CompilerParams(
             collective_id=0, has_side_effects=True, vmem_limit_bytes=48 * 1024 * 1024
         ),
         name="adjoint",
     )(
-        pref_rows.reshape(-1),
+        preference,
         base_mortality,
-        lead,
+        age_class,
+        blocked(final_adjoint),
         blocked(first_density),
         blocked(second_density),
         blocked(forage),
-        fields,
+        blocked(land_mask),
+        blocked(east_velocity),
+        blocked(north_velocity),
+        age_class.reshape(1, -1),
     )
-    onehot = (age_class[None, :] == jnp.arange(classes, dtype=jnp.int32)[:, None]).astype(f32)
-    local = jnp.dot(onehot, jnp.sum(grad, axis=2), precision=lax.Precision.HIGHEST)
-    cells = land_mask.shape[0] * tiles * land_mask.shape[1]
-    summed = lax.psum(local, "tile") / cells
+    summed = grad[0].reshape(groups, classes).T
     return (unblocked(out, rows), unblocked(sens, rows), summed)
 
 

time: 115 us -> 90.9 us (0.79)
  blocking collectives: 32.7 us -> 0 us
  Pallas kernels: 70.4 us -> 78.3 us
  local copies, waits for them, and re-layouts: 7.35 us -> 11.4 us
  other arithmetic: 3.05 us -> 0 us
    psum x1 -> x0, blocking collectives: 32.7 us -> none  [shards(): summed = lax.psum(local, 'tile') / cells]
    pallas_call x1, Pallas kernels: 70.4 us -> 78.3 us  [shards(): pl.pallas_call(body, out_shape=(jax.ShapeDtypeStruct((cohorts,) + cell, f...]
    unnamed x13 -> x21, local copies, waits for them, and re-layouts: 4.06 us -> 10.7 us
    slice x2 -> x1, local copies, waits for them, and re-layouts: 2.49 us -> 0.02 us  [shards(): summed = grad[0].reshape(groups, classes).T]
    another operation x2 -> x0, other arithmetic: 1.43 us -> none  [shards(): jnp.stack([land_mask.astype(jnp.float32), east_velocity, north_velocity])]
where the time goes in v2:
time: 90.9 us; the launch traced here: 90.4 us
  Pallas kernels  78.3 us (86%)
  local copies, waits for them, and re-layouts  11.4 us (13%)
    pallas_call x1, Pallas kernels, shards(): pl.pallas_call(body, out_shape=(jax.ShapeDtypeStruct((cohorts,) + cell, f...  78.3 us
    unnamed x21, local copies, waits for them, and re-layouts  10.7 us

profile of v2, /device:TPU:0, one launch (start us, length us, event | category | flops | bytes accessed | tf_op | source)
XLA Modules:
  0.0 90.4 jit_solution(12418977701452620301)
XLA Ops:
  0.6 0.8 copy.20.refs_0_
  1.4 0.0 copy-start
  1.4 1.3 %copy-done = f32[160,2,1024]{2,1,0:T(2,128)S(1)} copy-done((f32[160,2,1024]{2,1,0:T(2,128)S(1)}, f32[160,2,1024]{2,1,0:T(2,128)}, u32[]{:S(2)}) %copy-start) | copy-done | bytes 1310744
  2.7 0.0 copy-start.1
  2.7 1.3 %copy-done.1 = f32[160,2,1024]{2,1,0:T(2,128)S(1)} copy-done((f32[160,2,1024]{2,1,0:T(2,128)S(1)}, f32[160,2,1024]{2,1,0:T(2,128)}, u32[]{:S(2)}) %copy-start.1) | copy-done | bytes 1310744
  4.0 0.0 copy-start.2
  4.0 1.3 %copy-done.2 = f32[160,2,1024]{2,1,0:T(2,128)S(1)} copy-done((f32[160,2,1024]{2,1,0:T(2,128)S(1)}, f32[160,2,1024]{2,1,0:T(2,128)}, u32[]{:S(2)}) %copy-start.2) | copy-done | bytes 1310744
  5.3 0.0 copy-start.3
  5.3 0.9 copy-done.3
  6.2 0.0 copy-start.4
  6.2 0.7 copy-done.4
  6.9 0.0 copy-start.5
  6.9 0.7 copy-done.5
  7.6 0.0 copy-start.6
  7.6 0.7 copy-done.6
  8.3 0.0 copy-start.7
  8.3 0.7 copy-done.7
  9.0 0.0 copy-start.8
  9.0 0.7 copy-done.8
  9.7 78.3 %adjoint.1 = (f32[160,16,128]{2,1,0:T(8,128)S(1)}, f32[2,6,16,128]{3,2,1,0:T(8,128)S(1)}, f32[8,96]{1,0:T(8,128)S(1)}) custom-call(f32[16,6]{1,0:T(8,128)S(1)} %copy.20.refs_0_, f32[160]{0:T(256)S(1)} %copy-done.8, s32[160]{0:T(256)S(1)} %copy-done.7, f32[160,16,128]{2,1,0:T(8,128)S(1)} %bitcast.47, f32[160,16,128]{2,1,0:T(8,128)S(1)} %bitcast.48, ...), custom_call_target="tpu_custom_call" | custom-call | tf_op jit(solution)/shard_map/adjoint/pallas_call | solution.py:558
  88.1 0.7 reshape_squeeze.3
  88.7 1.1 %copy.25 = f32[160,2,1024]{2,1,0:T(2,128)} copy(f32[160,2,1024]{2,1,0:T(2,128)S(1)} %bitcast.50) | data formatting | bytes 2621440
  89.8 0.6 copy.26
  (1 shorter events, 0.0 us)
Async XLA Ops:
  1.4 1.3 %copy-start = (f32[160,2,1024]{2,1,0:T(2,128)S(1)}, f32[160,2,1024]{2,1,0:T(2,128)}, u32[]{:S(2)}) copy-start(f32[160,2,1024]{2,1,0:T(2,128)} %param.10) | copy-start | bytes 3932164
  2.7 1.3 %copy-start.1 = (f32[160,2,1024]{2,1,0:T(2,128)S(1)}, f32[160,2,1024]{2,1,0:T(2,128)}, u32[]{:S(2)}) copy-start(f32[160,2,1024]{2,1,0:T(2,128)} %param.11) | copy-start | bytes 3932164
  4.0 1.3 %copy-start.2 = (f32[160,2,1024]{2,1,0:T(2,128)S(1)}, f32[160,2,1024]{2,1,0:T(2,128)}, u32[]{:S(2)}) copy-start(f32[160,2,1024]{2,1,0:T(2,128)} %param.12) | copy-start | bytes 3932164
  5.3 0.9 copy-start.3
  6.2 0.7 copy-start.4
  6.9 0.7 copy-start.5
  7.6 0.7 copy-start.6
  8.3 0.7 copy-start.7
  9.0 0.7 copy-start.8

commit v3 on v2

--- a/solution.py
+++ b/solution.py
@@ -22,9 +22,9 @@
     base,
     cls,
     lead,
-    dens1,
-    dens2,
-    food,
+    dens1_in,
+    dens2_in,
+    food_in,
     mask_in,
     east_in,
     north_in,
@@ -46,8 +46,18 @@
     adem_all,
     short1,
     feed_sq,
-    surv,
+    dens1,
+    dens2,
+    food,
+    surv1,
+    surv2,
+    decay,
+    by_kind,
+    living,
+    adding,
+    crowd,
     grad,
+    by_class,
     near_sum,
     far_sum,
     lsend,
@@ -77,6 +87,7 @@
     tiles, group, cohorts, quarter, forage, chunks = dims
     half = group // 2
     blocks = food.shape[2]
+    classes = table.shape[1]
     me = lax.axis_index("tile")
     q = lax.rem(me, group)
     first = me - q
@@ -89,6 +100,13 @@
     def source(o):
         return lax.rem(q + group - o, group)
 
+    loads = [
+        pltpu.make_async_copy(src, dst, own_sem.at[3 + i])
+        for i, (src, dst) in enumerate(((dens2_in, dens2), (food_in, food), (dens1_in, dens1)))
+    ]
+    for copy in loads:
+        copy.start()
+
     barrier = pltpu.get_barrier_semaphore()
     for o in range(1, group):
         pl.semaphore_signal(barrier, inc=1, device_id={"tile": peer(o)}, device_id_type=MESH)
@@ -100,7 +118,7 @@
     pl.semaphore_wait(barrier, group + spans - 2)
 
     def pref(a, k):
-        return table[cls[a], k]
+        return table[k, cls[a]]
 
     def remote(src, dst, ssem, rsem, target):
         return pltpu.make_async_remote_copy(
@@ -218,21 +236,47 @@
 
     zero = jnp.zeros((blocks, LANES), jnp.float32)
 
-    def demands(dens):
-        def step(a, sums):
-            n = dens[a]
-            return tuple(sums[k] + pref(a, k) * n for k in range(forage))
-
-        return lax.fori_loop(0, cohorts, step, (zero,) * forage, unroll=4)
-
-    def prepare(month, dens, short_store):
-        sums = demands(dens)
+    kinds = lax.broadcasted_iota(jnp.int32, (classes, cohorts), 0)
+    onehot = (kinds == cls_row[...]).astype(jnp.float32)
+    high = lax.Precision.HIGHEST
+
+    def kind_sum(values):
+        return jnp.dot(onehot, values, precision=high, preferred_element_type=jnp.float32)
+
+    def prepare(month, dens, surv, short_store):
+        for r in range(blocks):
+            crowd[month, :, r, :] = kind_sum(dens[:, r, :])
+        shorts = []
         for k in range(forage):
+            hungry = table[k, 0] * crowd[month, 0]
+            for kind in range(1, classes):
+                hungry = hungry + table[k, kind] * crowd[month, kind]
             feed = food[month, k]
-            total = feed + sums[k]
-            short_store(k, sums[k] / total)
+            total = feed + hungry
+            shorts.append(hungry / total)
+            short_store(k, shorts[k])
             feed_sq[month, k] = feed / (total * total)
-            feed_sq[2 + month, k] = sums[k]
+            feed_sq[2 + month, k] = hungry
+        for kind in range(classes):
+            by_kind[kind] = jnp.exp(-weighted(kind, shorts))
+
+        def step(a, carry):
+            surv[a] = decay[a] * by_kind[cls[a]]
+            return carry
+
+        lax.fori_loop(0, cohorts, step, 0, unroll=4)
+
+    def weighted(kind, values):
+        total = table[0, kind] * values[0]
+        for k in range(1, forage):
+            total = total + table[k, kind] * values[k]
+        return total
+
+    def fade(a, carry):
+        decay[a] = jnp.exp(jnp.full((blocks, LANES), -base[a]))
+        return carry
+
+    lax.fori_loop(0, cohorts, fade, 0, unroll=4)
 
     def store_two(k, value):
         short_all[q, k] = value
@@ -240,7 +284,9 @@
     def store_one(k, value):
         short1[k] = value
 
-    prepare(1, dens2, store_two)
+    loads[0].wait()
+    loads[1].wait()
+    prepare(1, dens2, surv2, store_two)
     for o in range(1, group):
         gather_copy(short_all, ssend, srecv, o).start()
 
@@ -270,7 +316,8 @@
         south = jnp.where(odd, pltpu.roll(below, 1, 0), pltpu.roll(slots[s], blocks - 1, 0))
         return north, south
 
-    prepare(0, dens1, store_one)
+    loads[2].wait()
+    prepare(0, dens1, surv1, store_one)
 
     def lead_wait(c):
         for p in [c] if c < chunks - 1 else range(c, len(lead_parts)):
@@ -348,20 +395,18 @@
             out_copy(done2, aged2, o, c, osend, orecv).start()
         out_own(done2, aged2, c, orecv).start()
 
-    def ratio_part(lo, size, aged, dens, short, sums):
+    def ratio_part(lo, size, aged, dens, surv, sums, short=None):
         def step(a, sums):
-            level = base[a]
-            hunger = [pref(a, k) for k in range(forage)]
-            for k in range(forage):
-                level = level + hunger[k] * short[k]
-            kept = jnp.exp(-level)
-            surv[a] = kept
-            dying = aged[a] * kept * dens[a]
-            return tuple(sums[k] + hunger[k] * dying for k in range(forage))
+            dying = aged[a] * surv[a] * dens[a]
+            if short is not None:
+                for k in range(forage):
+                    row = jnp.sum(dying * short[k], axis=0, keepdims=True)
+                    grad[k, pl.ds(a, 1)] = grad[k, pl.ds(a, 1)] + row
+            return tuple(sums[k] + pref(a, k) * dying for k in range(forage))
 
         for part in range(group):
             start = part * quarter + lo
-            sums = lax.fori_loop(start, start + size, step, sums, unroll=2)
+            sums = lax.fori_loop(start, start + size, step, sums)
         return sums
 
     def finish(month, ratio):
@@ -371,29 +416,28 @@
             sens[month, k] = ratio[k] * feed_sq[2 + month, k] * feed_sq[month, k]
         return adem
 
-    def slopes(aged, dens, short, adem, add):
+    def slopes(aged, dens, surv, short):
         def step(a, carry):
-            n = dens[a]
-            dying = aged[a] * surv[a] * n
+            dying = aged[a] * surv[a] * dens[a]
             for k in range(forage):
-                both = n * adem[k] - dying * short[k]
-                row = jnp.sum(both, axis=0, keepdims=True)
-                if add:
-                    row = row + grad[k, pl.ds(a, 1)]
-                grad[k, pl.ds(a, 1)] = row
+                grad[k, pl.ds(a, 1)] = jnp.sum(dying * short[k], axis=0, keepdims=True)
             return carry
 
         lax.fori_loop(0, cohorts, step, 0, unroll=2)
 
-    def outgoing(aged, adem):
+    def outgoing(aged, surv, lo, hi):
         def step(a, carry):
-            total = aged[a] * surv[a]
-            for k in range(forage):
-                total = total + pref(a, k) * adem[k]
-            out[a] = total
+            out[a] = aged[a] * surv[a] + by_kind[cls[a]]
             return carry
 
-        lax.fori_loop(0, cohorts, step, 0, unroll=4)
+        lax.fori_loop(lo, hi, step, 0, unroll=4)
+
+    for o in range(1, group):
+        gather_wait(short_all, ssend, srecv, o)
+    for s in range(group):
+        shorts = [short_all[s, k] for k in range(forage)]
+        for kind in range(classes):
+            living[kind, s] = jnp.exp(-weighted(kind, shorts))
 
     short2 = [short_all[q, k] for k in range(forage)]
     ratio = (zero,) * forage
@@ -401,35 +445,46 @@
         for o in range(1, group):
             out_wait(aged2, o, c, osend, orecv)
         out_own(done2, aged2, c, orecv).wait()
-        ratio = ratio_part(*part_cuts[c], aged2, dens2, short2, ratio)
+        ratio = ratio_part(*part_cuts[c], aged2, dens2, surv2, ratio)
     adem2 = finish(1, ratio)
     for k in range(forage):
         adem_all[q, k] = adem2[k]
     for o in range(1, group):
         gather_copy(adem_all, asend, arecv, o).start()
     for o in range(1, group):
-        gather_wait(short_all, ssend, srecv, o)
-    for o in range(1, group):
         gather_wait(adem_all, asend, arecv, o)
+    for s in range(group):
+        adems = [adem_all[s, k] for k in range(forage)]
+        for kind in range(classes):
+            adding[kind, s] = weighted(kind, adems)
 
     for c in range(chunks):
         lo, size = part_cuts[c]
 
         def middle(i, carry):
             a = jnp.minimum(q * quarter + i + 1, cohorts - 1)
-            hunger = [pref(a, k) for k in range(forage)]
+            kind = cls[a]
+            fading = decay[a]
             for s in range(group):
-                level = base[a]
-                add = zero
-                for k in range(forage):
-                    level = level + hunger[k] * short_all[s, k]
-                    add = add + hunger[k] * adem_all[s, k]
-                wide1[half + s, i] = done2[s, i + 1] * jnp.exp(-level) + add
+                wide1[half + s, i] = done2[s, i + 1] * (fading * living[kind, s]) + adding[kind, s]
             return carry
 
         lax.fori_loop(lo, lo + size, middle, 0)
         halo_start(wide1, lo, size, z1send, z1recv, c)
-    slopes(aged2, dens2, short2, adem2, False)
+    slopes(aged2, dens2, surv2, short2)
+
+    def crowd_part(month, adem):
+        parts = []
+        for k in range(forage):
+            rows = [
+                jnp.sum(crowd[month, kind] * adem[k], axis=0, keepdims=True)
+                for kind in range(classes)
+            ]
+            parts.append(jnp.concatenate(rows, axis=0))
+        return parts
+
+    for k, part in enumerate(crowd_part(1, adem2)):
+        by_class[k] = part
 
     for c in range(chunks):
         halo_wait(wide1, *part_cuts[c], z1send, z1recv, c)
@@ -444,28 +499,25 @@
         for o in range(1, group):
             out_wait(aged1, o, c, o1send, o1recv)
         out_own(done1, aged1, c, o1recv).wait()
-        ratio = ratio_part(*part_cuts[c], aged1, dens1, short_one, ratio)
+        ratio = ratio_part(*part_cuts[c], aged1, dens1, surv1, ratio, short_one)
     adem1 = finish(0, ratio)
-    slopes(aged1, dens1, short_one, adem1, True)
-
-    classes = table.shape[0]
-    kinds = lax.broadcasted_iota(jnp.int32, (classes, cohorts), 0)
-    onehot = (kinds == cls_row[...]).astype(jnp.float32)
-    high = lax.Precision.HIGHEST
-    by_class = jnp.concatenate(
-        [
-            jnp.dot(onehot, grad[k], precision=high, preferred_element_type=jnp.float32)
-            for k in range(forage)
-        ],
-        axis=0,
-    )
+
     ones = jnp.ones((8, LANES), jnp.float32)
-    near_sum[q] = lax.dot_general(
-        ones, by_class, (((1,), (1,)), ((), ())), precision=high,
-        preferred_element_type=jnp.float32,
-    )
+    parts = crowd_part(0, adem1)
+    rows = []
+    for k in range(forage):
+        total = by_class[k] + parts[k] - kind_sum(grad[k])
+        lanes_sum = lax.dot_general(
+            ones, total, (((1,), (1,)), ((), ())), precision=high,
+            preferred_element_type=jnp.float32,
+        )
+        rows.append(lanes_sum[0:1])
+    near_sum[q] = jnp.concatenate(rows, axis=0)
     for o in range(1, group):
         gather_copy(near_sum, nsend, nrecv, o).start()
+    for kind in range(classes):
+        by_kind[kind] = weighted(kind, adem1)
+    outgoing(aged1, surv1, 0, cohorts // 2)
     for o in range(1, group):
         gather_wait(near_sum, nsend, nrecv, o)
     span = me // group
@@ -477,7 +529,7 @@
 
     for g in range(1, spans):
         far_copy(g).start()
-    outgoing(aged1, adem1)
+    outgoing(aged1, surv1, cohorts // 2, cohorts)
     for g in range(1, spans):
         spot = far_sum.at[lax.rem(span + spans - g, spans)]
         remote(spot, spot, tsend.at[g], trecv.at[g], lax.rem(me + g * group, tiles)).wait_recv()
@@ -539,7 +591,7 @@
     tiles = lax.axis_size("tile")
     group = 2 * SUBSTEPS // rows
     quarter = cohorts // group
-    chunks = 5
+    chunks = 8
     blocks = rows * columns // LANES
     f32 = jnp.float32
     dma = pltpu.SemaphoreType.DMA
@@ -560,9 +612,9 @@
         out_shape=(
             jax.ShapeDtypeStruct((cohorts,) + cell, f32),
             jax.ShapeDtypeStruct((2, groups) + cell, f32),
-            jax.ShapeDtypeStruct((8, groups * classes), f32),
+            jax.ShapeDtypeStruct((groups, classes), f32),
         ),
-        in_specs=[smem, smem, smem, hbm] + [vmem] * 7,
+        in_specs=[smem, smem, smem] + [hbm] * 7 + [vmem],
         out_specs=(vmem, vmem, vmem),
         scratch_shapes=[
             pltpu.VMEM((2 * group, quarter + 1) + cell, f32),
@@ -580,18 +632,28 @@
             pltpu.VMEM((groups,) + cell, f32),
             pltpu.VMEM((4, groups) + cell, f32),
             pltpu.VMEM((cohorts,) + cell, f32),
+            pltpu.VMEM((cohorts,) + cell, f32),
+            pltpu.VMEM((2, groups) + cell, f32),
+            pltpu.VMEM((cohorts,) + cell, f32),
+            pltpu.VMEM((cohorts,) + cell, f32),
+            pltpu.VMEM((cohorts,) + cell, f32),
+            pltpu.VMEM((classes,) + cell, f32),
+            pltpu.VMEM((classes, group) + cell, f32),
+            pltpu.VMEM((classes, group) + cell, f32),
+            pltpu.VMEM((2, classes) + cell, f32),
             pltpu.VMEM((groups, cohorts, LANES), f32),
-            pltpu.VMEM((group, 8, groups * classes), f32),
-            pltpu.VMEM((tiles // group, 8, groups * classes), f32),
+            pltpu.VMEM((groups, classes, LANES), f32),
+            pltpu.VMEM((group, groups, classes), f32),
+            pltpu.VMEM((tiles // group, groups, classes), f32),
         ]
         + [dma((group, chunks + 2))] * 2 + hop + pair + hop + pair + [dma((group, 3))] * 2
-        + [dma((2, 3))] * 2 + one + one + one + [dma((tiles // group,))] * 2 + [dma((3,))],
+        + [dma((2, 3))] * 2 + one + one + one + [dma((tiles // group,))] * 2 + [dma((6,))],
         compiler_params=pltpu.CompilerParams(
-            collective_id=0, has_side_effects=True, vmem_limit_bytes=48 * 1024 * 1024
+            collective_id=0, has_side_effects=True, vmem_limit_bytes=60 * 1024 * 1024
         ),
         name="adjoint",
     )(
-        preference,
+        preference.T,
         base_mortality,
         age_class,
         blocked(final_adjoint),
@@ -603,7 +665,7 @@
         blocked(north_velocity),
         age_class.reshape(1, -1),
     )
-    summed = grad[0].reshape(groups, classes).T
+    summed = grad.T
     return (unblocked(out, rows), unblocked(sens, rows), summed)
 
 

time: 90.9 us -> 82.6 us (0.909)
  local copies, waits for them, and re-layouts: 11.4 us -> 4.1 us
    unnamed x21 -> x7, local copies, waits for them, and re-layouts: 10.7 us -> 4.1 us
where the time goes in v3:
time: 82.6 us; the launch traced here: 82.4 us
  Pallas kernels  77.7 us (94%)
  local copies, waits for them, and re-layouts  4.1 us (5%)
    pallas_call x1, Pallas kernels, shards(): pl.pallas_call(body, out_shape=(jax.ShapeDtypeStruct((cohorts,) + cell, f...  77.7 us
    unnamed x7, local copies, waits for them, and re-layouts  4.1 us

profile of v3, /device:TPU:0, one launch (start us, length us, event | category | flops | bytes accessed | tf_op | source)
XLA Modules:
  0.0 82.4 jit_solution(7118101009442959677)
XLA Ops:
  0.6 77.7 %adjoint.1 = (f32[160,16,128]{2,1,0:T(8,128)}, f32[2,6,16,128]{3,2,1,0:T(8,128)}, f32[6,16]{1,0:T(8,128)}) custom-call(f32[6,16]{1,0:T(8,128)} %bitcast.57, f32[160]{0:T(256)} %refs_1_.1, s32[160]{0:T(256)} %refs_2_.1, f32[160,16,128]{2,1,0:T(8,128)} %bitcast.48, f32[160,16,128]{2,1,0:T(8,128)} %bitcast.49, f32[160,16,128]{2,1,0:T(8,128)} %bitcast.50, ...), custom_call_target="tpu_custom_call" | custom-call | tf_op jit(solution)/shard_map/adjoint/pallas_call | solution.py:610
  78.3 0.0 copy-start
  78.3 0.0 copy-start.1
  78.4 2.9 %copy.25 = f32[160,2,1024]{2,1,0:T(2,128)} copy(f32[160,2,1024]{2,1,0:T(2,128)} %bitcast.51) | data formatting | bytes 2621440
  81.2 0.0 copy-done
  81.2 0.6 copy.26
  81.9 0.0 copy-done.1
  81.9 0.6 copy.27
Async XLA Ops:
  78.3 2.9 %copy-start = (f32[2,6,16,128]{3,2,1,0:T(8,128)S(1)}, f32[2,6,16,128]{3,2,1,0:T(8,128)}, u32[]{:S(2)}) copy-start(f32[2,6,16,128]{3,2,1,0:T(8,128)} %get-tuple-element.7) | copy-start | bytes 294916
  78.3 3.5 %copy-start.1 = (f32[6,16]{1,0:T(8,128)S(1)}, f32[6,16]{1,0:T(8,128)}, u32[]{:S(2)}) copy-start(f32[6,16]{1,0:T(8,128)} %get-tuple-element.8) | copy-start | bytes 1156

commit v4 on v3

--- a/solution.py
+++ b/solution.py
@@ -276,7 +276,6 @@
         decay[a] = jnp.exp(jnp.full((blocks, LANES), -base[a]))
         return carry
 
-    lax.fori_loop(0, cohorts, fade, 0, unroll=4)
 
     def store_two(k, value):
         short_all[q, k] = value
@@ -284,11 +283,6 @@
     def store_one(k, value):
         short1[k] = value
 
-    loads[0].wait()
-    loads[1].wait()
-    prepare(1, dens2, surv2, store_two)
-    for o in range(1, group):
-        gather_copy(short_all, ssend, srecv, o).start()
 
     for f, (src, dst) in enumerate(strips):
         own_fields[f].wait()
@@ -316,8 +310,6 @@
         south = jnp.where(odd, pltpu.roll(below, 1, 0), pltpu.roll(slots[s], blocks - 1, 0))
         return north, south
 
-    loads[2].wait()
-    prepare(0, dens1, surv1, store_one)
 
     def lead_wait(c):
         for p in [c] if c < chunks - 1 else range(c, len(lead_parts)):
@@ -389,11 +381,21 @@
         if c + 1 < chunks:
             lead_wait(c + 1)
             halo_start(wide2, *lead_cuts[c + 1], zsend, zrecv, c + 1)
+        if c + 2 == chunks:
+            lax.fori_loop(0, cohorts, fade, 0, unroll=4)
+            loads[0].wait()
+            loads[1].wait()
+            prepare(1, dens2, surv2, store_two)
+            for o in range(1, group):
+                gather_copy(short_all, ssend, srecv, o).start()
         halo_wait(wide2, *lead_cuts[c], zsend, zrecv, c)
         transport(wide2, done2, *lead_cuts[c])
         for o in range(1, group):
             out_copy(done2, aged2, o, c, osend, orecv).start()
         out_own(done2, aged2, c, orecv).start()
+
+    loads[2].wait()
+    prepare(0, dens1, surv1, store_one)
 
     def ratio_part(lo, size, aged, dens, surv, sums, short=None):
         def step(a, sums):

time: 82.6 us -> 82.5 us (level)
  no operation moved by 1% of the time
where the time goes in v4:
time: 82.5 us; the launch traced here: 82.3 us
  Pallas kernels  77.5 us (94%)
  local copies, waits for them, and re-layouts  4.1 us (5%)
    pallas_call x1, Pallas kernels, shards(): pl.pallas_call(body, out_shape=(jax.ShapeDtypeStruct((cohorts,) + cell, f...  77.5 us
    unnamed x7, local copies, waits for them, and re-layouts  4.1 us

profile of v4, /device:TPU:0, one launch (start us, length us, event | category | flops | bytes accessed | tf_op | source)
XLA Modules:
  0.0 82.3 jit_solution(2287555827627040656)
XLA Ops:
  0.6 77.5 %adjoint.1 = (f32[160,16,128]{2,1,0:T(8,128)}, f32[2,6,16,128]{3,2,1,0:T(8,128)}, f32[6,16]{1,0:T(8,128)}) custom-call(f32[6,16]{1,0:T(8,128)} %bitcast.57, f32[160]{0:T(256)} %refs_1_.1, s32[160]{0:T(256)} %refs_2_.1, f32[160,16,128]{2,1,0:T(8,128)} %bitcast.48, f32[160,16,128]{2,1,0:T(8,128)} %bitcast.49, f32[160,16,128]{2,1,0:T(8,128)} %bitcast.50, ...), custom_call_target="tpu_custom_call" | custom-call | tf_op jit(solution)/shard_map/adjoint/pallas_call | solution.py:612
  78.2 0.0 copy-start
  78.2 0.0 copy-start.1
  78.2 2.9 %copy.25 = f32[160,2,1024]{2,1,0:T(2,128)} copy(f32[160,2,1024]{2,1,0:T(2,128)} %bitcast.51) | data formatting | bytes 2621440
  81.0 0.0 copy-done
  81.0 0.6 copy.26
  81.7 0.0 copy-done.1
  81.7 0.6 copy.27
Async XLA Ops:
  78.2 2.9 %copy-start = (f32[2,6,16,128]{3,2,1,0:T(8,128)S(1)}, f32[2,6,16,128]{3,2,1,0:T(8,128)}, u32[]{:S(2)}) copy-start(f32[2,6,16,128]{3,2,1,0:T(8,128)} %get-tuple-element.7) | copy-start | bytes 294916
  78.2 3.5 %copy-start.1 = (f32[6,16]{1,0:T(8,128)S(1)}, f32[6,16]{1,0:T(8,128)}, u32[]{:S(2)}) copy-start(f32[6,16]{1,0:T(8,128)} %get-tuple-element.8) | copy-start | bytes 1156
